TPU v7x, 512 devices: a whole 4x4x16 slice. The times are simulated.
512 devices in a mesh: ctx: 64 (over y, z), head: 8 (over x, core).
Axes of the slice: x: 4, y: 4, z: 16, core: 2. Of those that a mesh axis runs over, the one named last changes fastest.
Arguments:
- lin_query: bfloat16 [8192, 64, 128], P('ctx', 'head'), may hold values from -6 to 6
- lin_key: bfloat16 [8192, 64, 128], P('ctx', 'head'), may hold values from -6 to 6
- lin_value: bfloat16 [8192, 64, 128], P('ctx', 'head'), may hold values from -18 to 18
- log_decay: float32 [64, 8192], P('head', 'ctx'), may hold values from -1 to 0
- norm_gain: float32 [64, 128], P('head'), may hold values from 0.5 to 1.5
- attn_query: bfloat16 [8192, 64, 128], P('ctx', 'head'), may hold values from -30 to 30
- attn_key: bfloat16 [8192, 8, 128], P('ctx', 'head'), may hold values from -16 to 16
- attn_value: bfloat16 [8192, 8, 128], P('ctx', 'head'), may hold values from -6 to 6
Outputs:
- lin_out: bfloat16 [8192, 64, 128], P('ctx', 'head')
- attn_out: bfloat16 [8192, 64, 128], P('ctx', 'head')
All inputs are finite; a program needn't handle non-finite values.
Results may differ from a plain program's by a relative error of at most 0.0055.
Values may be sent and summed in bfloat16 or wider, within the bound.
No kernel may reach another device: no remote copies, remote signals or barrier semaphores. Data moves between devices by JAX's collectives and lax.ppermute only.
A program may use at most 192 MiB of HBM per device.

v0:
```python
import jax
import jax.numpy as jnp
from jax import lax
from jax.sharding import PartitionSpec as P

QUERY_HEADS = 64
HD = 128


def carried_in(x, axis, combine, identity):
    size, mine = (lax.axis_size(axis), lax.axis_index(axis))
    everything = jax.tree.map(lambda part: lax.all_gather(part, axis), x)
    start = jax.tree.map(
        lambda part, zero: jnp.broadcast_to(jnp.asarray(zero, part.dtype), part.shape), x, identity
    )

    def hop(k, before):
        reached = k < mine
        new = combine(before, jax.tree.map(lambda part: part[k], everything))
        return jax.tree.map(lambda a, b: jnp.where(reached, a, b), new, before)

    return lax.fori_loop(0, size, hop, start)


def act_round(values):
    return jax.nn.silu(values.astype(jnp.float32)).astype(jnp.bfloat16)


def chain_state(earlier, later):
    decay_early, state_early = earlier
    decay_late, state_late = later
    return (decay_early * decay_late, decay_late[:, None, None] * state_early + state_late)


def lightning(lin_query, lin_key, lin_value, log_decay, norm_gain):
    act_query = act_round(lin_query)
    act_key = act_round(lin_key)
    act_value = act_round(lin_value)
    token_position = jnp.arange(lin_query.shape[0])
    cumulative = jnp.cumsum(log_decay, axis=1)
    causal = token_position[:, None] >= token_position[None, :]
    spread = cumulative[:, :, None] - cumulative[:, None, :]
    decay_matrix = jnp.exp(jnp.where(causal[None], spread, -1e30))
    scores = jnp.einsum("thd,shd->hts", act_query, act_key, preferred_element_type=jnp.float32)
    weights = (scores * decay_matrix).astype(jnp.bfloat16)
    inner_part = jnp.einsum("hts,shd->thd", weights, act_value, preferred_element_type=jnp.float32)
    last_sum = cumulative[:, -1]
    key_factor = jnp.exp(last_sum[None, :] - cumulative.T)
    scaled_keys = (act_key.astype(jnp.float32) * key_factor[:, :, None]).astype(jnp.bfloat16)
    local_state = jnp.einsum(
        "shd,she->hde", scaled_keys, act_value, preferred_element_type=jnp.float32
    )
    identity = (jnp.ones_like(last_sum), jnp.zeros_like(local_state))
    prior_decay, prior_state = carried_in(
        (jnp.exp(last_sum), local_state), "ctx", chain_state, identity
    )
    outer_part = jnp.einsum(
        "thd,hde->the", act_query.astype(jnp.float32), prior_state, precision=lax.Precision.HIGHEST
    )
    mixed_out = inner_part + outer_part * jnp.exp(cumulative.T)[:, :, None]
    row_squares = jnp.sum(mixed_out * mixed_out, axis=(1, 2))
    total_squares = lax.psum(row_squares, "head")
    inverse = lax.rsqrt(total_squares / (QUERY_HEADS * HD) + 1e-06)
    return (mixed_out * inverse[:, None, None] * norm_gain[None]).astype(jnp.bfloat16)


def to_groups(query_rows, kv_local):
    rows = query_rows.shape[0]
    group = query_rows.shape[1] // kv_local
    shaped = query_rows.reshape(rows, kv_local, group, query_rows.shape[2]).transpose(1, 0, 2, 3)
    return shaped.reshape(kv_local, rows * group, query_rows.shape[2])


def from_groups(grouped, rows):
    kv_local = grouped.shape[0]
    group = grouped.shape[1] // rows
    shaped = grouped.reshape(kv_local, rows, group, grouped.shape[2]).transpose(1, 0, 2, 3)
    return shaped.reshape(rows, kv_local * group, grouped.shape[2])


def attend(state_now, group_query, positions, key_piece, value_piece):
    running_max, totals, accumulated = state_now
    scores = jnp.einsum(
        "gqd,pgd->gqp", group_query, key_piece, preferred_element_type=jnp.float32
    ) * HD ** (-0.5)
    key_pos = jnp.arange(key_piece.shape[0])
    visible = positions[:, None] >= key_pos[None, :]
    masked = jnp.where(visible[None], scores, -1e30)
    newest = jnp.maximum(running_max, jnp.max(masked, axis=2))
    prob_rows = jnp.where(visible[None], jnp.exp(scores - newest[:, :, None]), 0.0)
    totals = jnp.sum(prob_rows, axis=2)
    accumulated = jnp.einsum(
        "gqp,pgd->gqd",
        prob_rows.astype(jnp.bfloat16),
        value_piece,
        preferred_element_type=jnp.float32,
    )
    return (newest, totals, accumulated)


def softmax_part(attn_query, attn_key, attn_value):
    length = attn_query.shape[0]
    kv_local = attn_key.shape[1]
    group = attn_query.shape[1] // kv_local
    ctx_index = lax.axis_index("ctx")
    own_pos = ctx_index * length + jnp.arange(length)
    query_sets = [(to_groups(attn_query, kv_local), jnp.repeat(own_pos, group), length)]

    def empty_state(group_query):
        shape_rows = group_query.shape[:2]
        return (
            jnp.full(shape_rows, -1e30, jnp.float32),
            jnp.zeros(shape_rows, jnp.float32),
            jnp.zeros(group_query.shape, jnp.float32),
        )

    initial = tuple((empty_state(query_set[0]) for query_set in query_sets))
    key_piece = lax.all_gather(attn_key, "ctx", axis=0, tiled=True)
    value_piece = lax.all_gather(attn_value, "ctx", axis=0, tiled=True)
    results = []
    for query_set, state_now in zip(query_sets, initial):
        group_query, positions, set_rows = query_set
        state_now = attend(state_now, group_query, positions, key_piece, value_piece)
        results.append(state_now)
    finals = tuple(results)
    running_max, totals, accumulated = finals[0]
    grouped = (accumulated / totals[:, :, None]).astype(jnp.bfloat16)
    result = from_groups(grouped, length)
    return result


def local(lin_query, lin_key, lin_value, log_decay, norm_gain, attn_query, attn_key, attn_value):
    lin_out = lightning(lin_query, lin_key, lin_value, log_decay, norm_gain)
    attn_out = softmax_part(attn_query, attn_key, attn_value)
    return (lin_out, attn_out)


def solution(mesh):
    return jax.shard_map(
        local,
        mesh=mesh,
        in_specs=(
            P("ctx", "head", None),
            P("ctx", "head", None),
            P("ctx", "head", None),
            P("head", "ctx"),
            P("head", None),
            P("ctx", "head", None),
            P("ctx", "head", None),
            P("ctx", "head", None),
        ),
        out_specs=(P("ctx", "head", None), P("ctx", "head", None)),
        check_vma=False,
    )
```

profile of v0, /device:TPU:1, one launch (start us, length us, event | category | flops | bytes accessed | tf_op | source)
XLA Modules:
  0.0 689.5 jit_solution(787471788955299901)
XLA Ops:
  10.0 1.4 multiply_convert_fusion.1
  12.5 1.3 dynamic-slice
  14.7 123.1 %all-reduce = f32[512]{0:T(512)S(1)} all-reduce(f32[512]{0:T(512)S(1)} %dynamic-update-slice), channel_id=2, replica_groups=mesh['ctx'=64,'head'=8] {'ctx'}, use_global_device_ids=true, to_apply=%add | all-reduce | flops 512 | bytes 4096
  139.3 9.0 %all-gather.6.cloned.1.call-done = bf16[8192,1,128]{2,0,1:T(8,128)(2,1)} async-done(((bf16[128,1,128]{2,0,1:T(8,128)(2,1)}), bf16[8192,1,128]{2,0,1:T(8,128)(2,1)}) %all-gather.6.cloned.1.call-update) | async-done | bytes 2097168 | tf_op jit(solution)/shard_map/all_gather | solution.py:118
  148.3 15.5 %select_reduce_fusion = (f32[1024]{0:T(1024)S(1)}, f32[1024,8192]{1,0:T(8,128)}) fusion(s32[1024]{0:T(1024)S(1)} %ge.35, bf16[8192,1,128]{2,0,1:T(8,128)(2,1)} %all-gather.6.cloned.1.call-done, bf16[128,8,128]{2,1,0:T(8,128)(2,1)S(1)} %copy-done), kind=kOutput, calls=%fused_computation.4 | convolution fusion | flops 2181037056 | bytes 35921920 | tf_op jit(solution)/shard_map/gqd,pgd->gqp/dot_general | solution.py:83
  163.8 15.6 %fusion.1 = f32[1024]{0:T(1024)S(1)} fusion(f32[1024,8192]{1,0:T(8,128)} %get-tuple-element.140, f32[1024]{0:T(1024)S(1)} %broadcast_maximum_fusion, s32[1024]{0:T(1024)S(1)} %ge.35), kind=kLoop, calls=%fused_computation.6 | loop fusion | flops 41942016 | bytes 33566720 | tf_op jit(solution)/shard_map/reduce_sum | solution.py:91
  179.4 108.9 %all-gather.8.cloned.1.call-done = bf16[8192,1,128]{2,0,1:T(8,128)(2,1)} async-done(((bf16[128,1,128]{2,0,1:T(8,128)(2,1)}), bf16[8192,1,128]{2,0,1:T(8,128)(2,1)}) %all-gather.8.cloned.1.call-update) | async-done | bytes 2097168 | tf_op jit(solution)/shard_map/all_gather | solution.py:119
  288.3 15.6 %fusion.21 = bf16[128,8,128]{2,1,0:T(8,128)(2,1)} fusion(bf16[8192,1,128]{2,0,1:T(8,128)(2,1)} %all-gather.8.cloned.1.call-done, f32[1024,8192]{1,0:T(8,128)} %get-tuple-element.140, f32[1024]{0:T(1024)S(1)} %broadcast_maximum_fusion, s32[1024]{0:T(1024)S(1)} %ge.35, f32[1024]{0:T(1024)S(1)} %fusion.1), kind=kOutput, calls=%fused_computation.20 | convolution fusion | flops 2189688832 | bytes 35926016 | tf_op jit(solution)/shard_map/gqp,pgd->gqd/dot_general | solution.py:92
  303.8 286.3 %all-gather.10.cloned.1.call-done = f32[512,128,128]{2,1,0:T(8,128)} async-done(((f32[8,128,128]{2,1,0:T(8,128)}), f32[512,128,128]{2,1,0:T(8,128)}) %all-gather.10.cloned.1.call-update) | async-done | bytes 33554448 | tf_op jit(solution)/shard_map/all_gather | solution.py:12
  590.1 77.7 %while.14 = (s32[]{:T(128)}, f32[8,128,128]{2,1,0:T(8,128)S(1)}, s32[]{:T(128)}, f32[64,8]{1,0:T(8,128)S(1)}, f32[64,8,128,128]{3,2,1,0:T(8,128)}, /*index=5*/s32[]{:T(128)}, s32[]{:T(128)}) while((s32[]{:T(128)}, f32[8,128,128]{2,1,0:T(8,128)S(1)}, s32[]{:T(128)}, f32[64,8]{1,0:T(8,128)S(1)}, f32[64,8,128,128]{3,2,1,0:T(8,128)}, ...), condition=%wide.region_2.3_spmd.clone, body=%wide.region_1.2_spmd.clone.sunk | while | flops 524292 | bytes 1573065 | solution.py:22
  591.4 1.2 fusion.65
  592.6 1.2 fusion.65
  593.8 1.2 fusion.65
  595.0 1.2 fusion.65
  596.2 1.2 fusion.65
  597.4 1.2 fusion.65
  598.6 1.2 fusion.65
  599.9 1.2 fusion.65
  602.3 1.2 fusion.65
  604.7 1.2 fusion.65
  605.9 1.2 fusion.65
  607.1 1.2 fusion.65
  608.4 1.2 fusion.65
  609.6 1.2 fusion.65
  610.8 1.2 fusion.65
  612.0 1.2 fusion.65
  613.2 1.2 fusion.65
  614.4 1.2 fusion.65
  615.6 1.2 fusion.65
  616.8 1.2 fusion.65
  618.1 1.2 fusion.65
  619.3 1.2 fusion.65
  620.5 1.2 fusion.65
  621.7 1.2 fusion.65
  622.9 1.2 fusion.65
  625.3 1.2 fusion.65
  627.8 1.2 fusion.65
  629.0 1.2 fusion.65
  630.2 1.2 fusion.65
  631.4 1.2 fusion.65
  632.6 1.2 fusion.65
  633.8 1.2 fusion.65
  635.1 1.2 fusion.65
  636.3 1.2 fusion.65
  637.5 1.2 fusion.65
  638.7 1.2 fusion.65
  639.9 1.2 fusion.65
  669.0 12.9 %psum.7 = f32[128]{0:T(128)S(1)} all-reduce(f32[128]{0:T(128)S(1)} %get-tuple-element.137), channel_id=1, replica_groups=mesh['ctx'=64,'head'=8] {'head'}, use_global_device_ids=true, to_apply=%region_4.5 | all-reduce | flops 128 | bytes 1024 | tf_op jit(solution)/shard_map/psum | solution.py:62
  (123 shorter events, 40.1 us)
Async XLA Ops:
  7.2 141.1 %copy-start = (bf16[128,8,128]{2,1,0:T(8,128)(2,1)S(1)}, bf16[128,8,128]{2,1,0:T(8,128)(2,1)}, u32[]{:S(2)}) copy-start(bf16[128,8,128]{2,1,0:T(8,128)(2,1)} %param.15) | copy-start | bytes 786436
  7.2 141.1 %all-gather.6.cloned.1.call-start = ((), (), s32[]{:S(2)}) async-start(), calls=%async_computation | async-start | bytes 2129920 | tf_op jit(solution)/shard_map/all_gather | solution.py:118
  7.9 280.4 %all-gather.8.cloned.1.call-start = ((), (), s32[]{:S(2)}) async-start(), calls=%async_computation.1 | async-start | bytes 2129920 | tf_op jit(solution)/shard_map/all_gather | solution.py:119
  8.7 581.5 %all-gather.10.cloned.1.call-start = ((), (), s32[]{:S(2)}) async-start(), calls=%async_computation.2 | async-start | bytes 34078720 | tf_op jit(solution)/shard_map/all_gather | solution.py:12
  163.8 519.2 %copy-start.1 = (bf16[128,8,128]{2,1,0:T(8,128)(2,1)S(1)}, bf16[128,8,128]{2,1,0:T(8,128)(2,1)}, u32[]{:S(2)}) copy-start(bf16[128,8,128]{2,1,0:T(8,128)(2,1)} %param.15) | copy-start | bytes 786436
  179.4 502.4 %copy-start.2 = (f32[8,128]{1,0:T(8,128)S(1)}, f32[8,128]{1,0:T(8,128)}, u32[]{:S(2)}) copy-start(f32[8,128]{1,0:T(8,128)} %param.14) | copy-start | bytes 12292
Sparse Core Ops, SparseCore 0:
  11.0 137.2 all-gather.5
  151.2 136.9 all-gather.7
  291.2 298.8 all-gather.9
where the time goes:
time: 693 us; the launch traced here: 689 us
  waiting for transfers between devices  406 us (59%)
  blocking collectives  136 us (20%)
  other arithmetic  94.4 us (14%)
  matrix products  33.2 us (5%)
  between operations  14.5 us (2%)
    all_gather x1, waiting for transfers between devices, carried_in(): everything = jax.tree.map(lambda part: lax.all_gather(part, axis), x)  286 us
    unnamed x1, blocking collectives  123 us
    all_gather x1, waiting for transfers between devices, softmax_part(): value_piece = lax.all_gather(attn_value, 'ctx', axis=0, tiled=True)  109 us
    select_n x64, other arithmetic, hop(): return jax.tree.map(lambda a, b: jnp.where(reached, a, b), new, before)  75.1 us
    reduce_sum x1, other arithmetic, attend(): totals = jnp.sum(prob_rows, axis=2)  15.6 us
    dot_general x1, matrix products, attend(): jnp.einsum('gqp,pgd->gqd', prob_rows.astype(jnp.bfloat16), value_piece, p...  15.6 us
    dot_general x1, matrix products, attend(): jnp.einsum('gqd,pgd->gqp', group_query, key_piece, preferred_element_type...  15.5 us
  transfers between devices with their start and end apart: 3, of which 3 were waited for; matrix products, arithmetic and copies ran while one was open for 8% of the time, Pallas kernels for 0%

commit v1 on v0

v1 whole, which is shorter than its diff:
```python
import jax
import jax.numpy as jnp
from jax import lax
from jax.experimental import pallas as pl
from jax.experimental.pallas import tpu as pltpu
from jax.sharding import PartitionSpec as P

QUERY_HEADS = 64
HD = 128
TOK = 128
HEADS = 8
ROWS = TOK * HEADS
Y, Z = 4, 16
SLICE = ROWS // Z
STATE_ROWS = SLICE + 16
STAT_ROWS = 32
LOG2E = 1.4426950408889634
SCALE2 = LOG2E * HD ** (-0.5)
NEG = -1e30
F32, BF16 = jnp.float32, jnp.bfloat16
Z_GROUPS = [[y * Z + z for z in range(Z)] for y in range(Y)]
Y_GROUPS = [[y * Z + z for y in range(Y)] for z in range(Z)]


def split3(x):
    high = x.astype(BF16)
    rest = x - high.astype(F32)
    mid = rest.astype(BF16)
    low = (rest - mid.astype(F32)).astype(BF16)
    return high, mid, low


def scalar_rows(x):
    high, mid, low = (part.astype(F32) for part in split3(x))
    row = lax.broadcasted_iota(jnp.int32, (16, 128), 0)
    out = jnp.where(row == 0, high, jnp.where(row == 1, mid, jnp.where(row == 2, low, 0.0)))
    return out.astype(BF16)


def scalar_back(rows):
    rows = rows.astype(F32)
    return rows[0:1] + rows[1:2] + rows[2:3]


def silu(ref):
    x = ref[...].astype(F32)
    return x / (1.0 + jnp.exp(-x))


def local_kernel(q_ref, k_ref, v_ref, decay_ref, pay_ref, inner_ref, act_ref, ecum_ref, sq, sk, sv):
    sq[...] = silu(q_ref)
    sk[...] = silu(k_ref)
    sv[...] = silu(v_ref)
    lane = lax.broadcasted_iota(jnp.int32, (HEADS, TOK), 1)
    cum = decay_ref[...]
    step = 1
    while step < TOK:
        cum = cum + jnp.where(lane >= step, pltpu.roll(cum, step, 1), 0.0)
        step *= 2
    cum_col = jnp.transpose(jnp.concatenate([cum] * (TOK // HEADS), axis=0))
    ecum_ref[...] = jnp.exp(cum_col)
    causal = lax.broadcasted_iota(jnp.int32, (TOK, TOK), 0) >= lax.broadcasted_iota(
        jnp.int32, (TOK, TOK), 1
    )
    for h in range(HEADS):
        mine = pl.ds(h, TOK, stride=HEADS)
        aq = sq[mine, :].astype(BF16)
        ak = sk[mine, :].astype(BF16)
        av = sv[mine, :].astype(BF16)
        act_ref[h] = aq
        row = cum[h : h + 1, :]
        col = cum_col[:, h : h + 1]
        last = row[:, TOK - 1 : TOK]
        scores = lax.dot_general(aq, ak, (((1,), (1,)), ((), ())), preferred_element_type=F32)
        weights = (scores * jnp.exp(jnp.where(causal, col - row, NEG))).astype(BF16)
        inner_ref[h] = jnp.dot(weights, av, preferred_element_type=F32)
        scaled = (ak.astype(F32) * jnp.exp(last - col)).astype(BF16)
        state = lax.dot_general(scaled, av, (((0,), (0,)), ((), ())), preferred_element_type=F32)
        extra = scalar_rows(jnp.broadcast_to(last, (1, 128)))
        for half in range(2):
            pay_ref[2 * h + half, 0:SLICE, :] = state[half * SLICE : (half + 1) * SLICE].astype(BF16)
            pay_ref[2 * h + half, SLICE:STATE_ROWS, :] = extra


def row_kernel(got_ref, q_ref, before_ref, lead_ref, pay_ref):
    run = jnp.zeros((SLICE, 128), F32)
    total = jnp.zeros((1, 128), F32)
    for z in range(Z):
        before_ref[z] = run
        lead_ref[z : z + 1, :] = total
        decay = scalar_back(got_ref[z, SLICE:STATE_ROWS, :])
        run = run * jnp.exp(decay) + got_ref[z, 0:SLICE, :].astype(F32)
        total = total + decay
    extra = scalar_rows(total)
    for y in range(Y):
        pay_ref[y, 0:SLICE, :] = run.astype(BF16)
        pay_ref[y, SLICE:STATE_ROWS, :] = extra
        pay_ref[y, STATE_ROWS:, :] = q_ref[...]


def carry_kernel(pos_ref, got_ref, before_ref, lead_ref, out_ref):
    mine = pos_ref[0]
    carry = jnp.zeros((SLICE, 128), F32)
    for y in range(Y - 1):
        decay = scalar_back(got_ref[y, SLICE:STATE_ROWS, :])
        new = carry * jnp.exp(decay) + got_ref[y, 0:SLICE, :].astype(F32)
        carry = jnp.where(y < mine, new, carry)
    for z in range(Z):
        out_ref[z] = (before_ref[z] + jnp.exp(lead_ref[z : z + 1, :]) * carry).astype(BF16)


def mix_kernel(act_ref, inner_ref, ecum_ref, prior_ref, mixed_ref, square_ref):
    squares = jnp.zeros((TOK, HD), F32)
    for h in range(HEADS):
        outer = jnp.dot(act_ref[h], prior_ref[h * HD : (h + 1) * HD, :], preferred_element_type=F32)
        mixed = inner_ref[h] + outer * ecum_ref[:, h : h + 1]
        squares = squares + mixed * mixed
        mixed_ref[pl.ds(h, TOK, stride=HEADS), :] = mixed
    square_ref[...] = jnp.sum(jnp.transpose(squares), axis=0, keepdims=True)


QT = 256
KEYS = Z * TOK


def attend_kernel(pos_ref, got_ref, kv_ref, out_ref, keys, vaug, stats):
    my_y, my_z = pos_ref[0], pos_ref[1]
    for z in range(Z):
        keys[z * TOK : (z + 1) * TOK, :] = kv_ref[z, 0:TOK, :]
        vaug[z * TOK : (z + 1) * TOK, 0:HD] = kv_ref[z, TOK : 2 * TOK, :]
    vaug[:, HD:] = jnp.ones((KEYS, HD), BF16)

    def tile(y, i, masked):
        start = pl.multiple_of(i * QT, QT)
        q = got_ref[y, pl.ds(STATE_ROWS + start, QT), :]
        s = lax.dot_general(q, keys[...], (((1,), (1,)), ((), ())), preferred_element_type=F32)
        if masked:
            row = lax.broadcasted_iota(jnp.int32, (QT, KEYS), 0)
            key = lax.broadcasted_iota(jnp.int32, (QT, KEYS), 1)
            pos = my_z * TOK + (row + start) // HEADS
            s = jnp.where(pos >= key, s, NEG)
        top = jnp.max(s, axis=1, keepdims=True) * SCALE2
        p = jnp.exp2(s * SCALE2 - top).astype(BF16)
        acc = jnp.dot(p, vaug[...], preferred_element_type=F32)
        total = acc[:, HD:]
        out_ref[y, pl.ds(STAT_ROWS + start, QT), :] = (acc[:, :HD] / total).astype(BF16)
        lse = top + jnp.log(total) * LOG2E
        for b in range(QT // 128):
            stats[pl.ds(i * (QT // 128) + b, 1), :] = jnp.transpose(lse[b * 128 : (b + 1) * 128])[0:1]

    for y in range(Y):

        @pl.when(my_y < y)
        def _():
            lax.fori_loop(0, ROWS // QT, lambda i, c: (tile(y, i, False), c)[1], 0)

        @pl.when(my_y == y)
        def _():
            lax.fori_loop(0, ROWS // QT, lambda i, c: (tile(y, i, True), c)[1], 0)

        @pl.when(my_y > y)
        def _():
            stats[...] = jnp.full((HEADS, 128), NEG, F32)
            out_ref[y, STAT_ROWS:, :] = jnp.zeros((ROWS, HD), BF16)

        high, mid, low = split3(stats[...])
        zero = jnp.zeros((HEADS, 128), BF16)
        out_ref[y, 0:16, :] = jnp.concatenate([high, mid], axis=0)
        out_ref[y, 16:32, :] = jnp.concatenate([low, zero], axis=0)


def merge_kernel(got_ref, out_ref):
    lse = []
    for y in range(Y):
        first = got_ref[y, 0:16, :].astype(F32)
        second = got_ref[y, 16:32, :].astype(F32)
        lse.append(first[0:8] + first[8:16] + second[0:8])
    top = jnp.maximum(jnp.maximum(lse[0], lse[1]), jnp.maximum(lse[2], lse[3]))
    w = [jnp.exp2(x - top) for x in lse]
    total = w[0] + w[1] + w[2] + w[3]
    w = [x / total for x in w]
    for b in range(ROWS // 128):
        rows = slice(STAT_ROWS + b * 128, STAT_ROWS + (b + 1) * 128)
        acc = jnp.zeros((128, HD), F32)
        for y in range(Y):
            col = jnp.transpose(jnp.broadcast_to(w[y][b : b + 1, :], (128, 128)))
            acc = acc + col * got_ref[y, rows, :].astype(F32)
        out_ref[b * 128 : (b + 1) * 128, :] = acc.astype(BF16)


def shape(*dims, kind=BF16):
    return jax.ShapeDtypeStruct(dims, kind)


VM = pl.BlockSpec(memory_space=pltpu.VMEM)
SM = pl.BlockSpec(memory_space=pltpu.SMEM)


def params(mib=16):
    return pltpu.CompilerParams(vmem_limit_bytes=mib << 20)


def cost(flops, nbytes, exps=0):
    return pl.CostEstimate(flops=flops, bytes_accessed=nbytes, transcendentals=exps)


def local(lin_query, lin_key, lin_value, log_decay, norm_gain, attn_query, attn_key, attn_value):
    index = lax.axis_index("ctx")
    pos = jnp.stack([index // Z, index % Z]).astype(jnp.int32)

    kv = jnp.concatenate([attn_key.reshape(TOK, HD), attn_value.reshape(TOK, HD)], axis=0)
    kv_row = lax.all_gather(kv, "ctx", axis_index_groups=Z_GROUPS)

    flat = lambda x: x.reshape(ROWS, HD)
    pay, inner, act, ecum = pl.pallas_call(
        local_kernel,
        out_shape=(
            shape(Z, STATE_ROWS, 128),
            shape(HEADS, TOK, HD, kind=F32),
            shape(HEADS, TOK, HD),
            shape(TOK, 128, kind=F32),
        ),
        in_specs=[VM] * 4,
        out_specs=(VM,) * 4,
        scratch_shapes=[pltpu.VMEM((ROWS, HD), F32)] * 3,
        compiler_params=params(),
        cost_estimate=cost(4 * 2 * 8 * 128**3, 2 << 20, 1 << 19),
        name="local_part",
    )(flat(lin_query), flat(lin_key), flat(lin_value), log_decay)
    got = lax.all_to_all(pay, "ctx", 0, 0, axis_index_groups=Z_GROUPS)

    before, lead, pay = pl.pallas_call(
        row_kernel,
        out_shape=(
            shape(Z, SLICE, 128, kind=F32),
            shape(Z, 128, kind=F32),
            shape(Y, STATE_ROWS + ROWS, 128),
        ),
        in_specs=[VM] * 2,
        out_specs=(VM,) * 3,
        compiler_params=params(),
        cost_estimate=cost(1 << 19, 3 << 20),
        name="row_scan",
    )(got, flat(attn_query))
    got = lax.all_to_all(pay, "ctx", 0, 0, axis_index_groups=Y_GROUPS)

    pay = pl.pallas_call(
        carry_kernel,
        out_shape=shape(Z, SLICE, 128),
        grid=(1,),
        in_specs=[
            SM,
            pl.BlockSpec((Y, STATE_ROWS, 128), lambda i: (0, 0, 0)),
            pl.BlockSpec((Z, SLICE, 128), lambda i: (0, 0, 0)),
            pl.BlockSpec((Z, 128), lambda i: (0, 0)),
        ],
        out_specs=pl.BlockSpec((Z, SLICE, 128), lambda i: (0, 0, 0)),
        compiler_params=params(),
        cost_estimate=cost(1 << 19, 1 << 20),
        name="carry_in",
    )(pos, got, before, lead)
    prior = lax.all_to_all(pay, "ctx", 0, 0, axis_index_groups=Z_GROUPS)

    mixed, squares = pl.pallas_call(
        mix_kernel,
        out_shape=(shape(ROWS, HD, kind=F32), shape(1, TOK, kind=F32)),
        in_specs=[VM] * 4,
        out_specs=(VM,) * 2,
        compiler_params=params(),
        cost_estimate=cost(2 * 8 * 128**3, 2 << 20),
        name="mix",
    )(act, inner, ecum, prior.reshape(ROWS, HD))
    total = lax.psum(squares, "head")
    inverse = lax.rsqrt(total[0] / (QUERY_HEADS * HD) + 1e-06)
    lin_out = mixed.reshape(TOK, HEADS, HD) * inverse[:, None, None] * norm_gain[None]
    lin_out = lin_out.astype(BF16)

    got, squares = lax.optimization_barrier((got, squares))
    pay = pl.pallas_call(
        attend_kernel,
        out_shape=shape(Y, STAT_ROWS + ROWS, HD),
        in_specs=[SM, VM, VM],
        out_specs=VM,
        scratch_shapes=[
            pltpu.VMEM((KEYS, HD), BF16),
            pltpu.VMEM((KEYS, 2 * HD), BF16),
            pltpu.VMEM((HEADS, 128), F32),
        ],
        compiler_params=params(40),
        cost_estimate=cost(3 * 2 * 4 * ROWS * KEYS * HD, 4 << 20, 4 * ROWS * KEYS),
        name="attend",
    )(pos, got, kv_row)
    got = lax.all_to_all(pay, "ctx", 0, 0, axis_index_groups=Y_GROUPS)
    attn_out = pl.pallas_call(
        merge_kernel,
        out_shape=shape(ROWS, HD),
        in_specs=[VM],
        out_specs=VM,
        compiler_params=params(),
        cost_estimate=cost(1 << 20, 2 << 20),
        name="merge",
    )(got)
    return lin_out, attn_out.reshape(TOK, HEADS, HD)


def solution(mesh):
    act = P("ctx", "head", None)
    return jax.shard_map(
        local,
        mesh=mesh,
        in_specs=(act, act, act, P("head", "ctx"), P("head", None), act, act, act),
        out_specs=(act, act),
        check_vma=False,
    )
```

time: 693 us -> 162 us (0.23)
  waiting for transfers between devices: 406 us -> 33.9 us
  other arithmetic: 94.4 us -> 1.63 us
  blocking collectives: 136 us -> 52.2 us
  matrix products: 33.2 us -> 0 us
  Pallas kernels: 0 us -> 30.9 us
  starting transfers between devices: 0.11 us -> 23.6 us
    all_gather x3 -> x1, waiting for transfers between devices: 404 us -> 9.25 us  [local(): kv_row = lax.all_gather(kv, 'ctx', axis_index_groups=Z_GROUPS)]
    unnamed x1 -> x0, blocking collectives: 123 us -> none
    select_n x64 -> x0, other arithmetic: 75.1 us -> none  [hop(): return jax.tree.map(lambda a, b: jnp.where(reached, a, b), new, before)]
    dot_general x5 -> x0, matrix products: 33.2 us -> none  [the longest x1 15.6 us: attend(): jnp.einsum('gqp,pgd->gqd', prob_rows.astype(jnp.bfloat16), value_piece, p...]
    pallas_call x0 -> x6, Pallas kernels: none -> 30.9 us  [the longest x1 24.9 us: local(): pl.pallas_call(attend_kernel, out_shape=shape(Y, STAT_ROWS + ROWS, HD), i...]
    all_to_all x0 -> x1, blocking collectives: none -> 29.4 us  [local(): prior = lax.all_to_all(pay, 'ctx', 0, 0, axis_index_groups=Z_GROUPS)]
    all_to_all x0 -> x3, waiting for transfers between devices: none -> 24.6 us  [the longest x1 14.5 us: local(): got = lax.all_to_all(pay, 'ctx', 0, 0, axis_index_groups=Z_GROUPS)]
    all_to_all x0 -> x3, starting transfers between devices: none -> 23.6 us  [the longest x1 15.7 us: local(): got = lax.all_to_all(pay, 'ctx', 0, 0, axis_index_groups=Z_GROUPS)]
  transfers between devices with their start and end apart: 3 -> 4, of which waited for: 3 -> 3; matrix products, arithmetic and copies ran while one was open for 8% -> 1% of each run, Pallas kernels for 0% -> 1%
where the time goes in v1:
time: 162 us; the launch traced here: 161 us
  blocking collectives  52.2 us (32%)
  waiting for transfers between devices  33.9 us (21%)
  Pallas kernels  30.9 us (19%)
  starting transfers between devices  23.6 us (15%)
  between operations  14.1 us (9%)
  local copies, waits for them, and re-layouts  4.81 us (3%)
  other arithmetic  1.63 us (1%)
    all_to_all x1, blocking collectives, local(): prior = lax.all_to_all(pay, 'ctx', 0, 0, axis_index_groups=Z_GROUPS)  29.4 us
    pallas_call x1, Pallas kernels, local(): pl.pallas_call(attend_kernel, out_shape=shape(Y, STAT_ROWS + ROWS, HD), i...  24.9 us
    psum x1, blocking collectives, local(): total = lax.psum(squares, 'head')  22.8 us
    all_to_all x1, starting transfers between devices, local(): got = lax.all_to_all(pay, 'ctx', 0, 0, axis_index_groups=Z_GROUPS)  15.7 us
    all_to_all x1, waiting for transfers between devices, local(): got = lax.all_to_all(pay, 'ctx', 0, 0, axis_index_groups=Z_GROUPS)  14.5 us
    all_to_all x2, waiting for transfers between devices, local(): got = lax.all_to_all(pay, 'ctx', 0, 0, axis_index_groups=Y_GROUPS)  10.1 us
    all_gather x1, waiting for transfers between devices, local(): kv_row = lax.all_gather(kv, 'ctx', axis_index_groups=Z_GROUPS)  9.25 us
    all_to_all x2, starting transfers between devices, local(): got = lax.all_to_all(pay, 'ctx', 0, 0, axis_index_groups=Y_GROUPS)  7.83 us
  transfers between devices with their start and end apart: 4, of which 3 were waited for; matrix products, arithmetic and copies ran while one was open for 1% of the time, Pallas kernels for 1%

profile of v1, /device:TPU:1, one launch (start us, length us, event | category | flops | bytes accessed | tf_op | source)
XLA Modules:
  0.0 161.1 jit_solution(8245851651617223434)
XLA Ops:
  7.2 0.0 copy-start
  7.2 0.0 copy-start.2
  7.2 1.0 copy-done.2
  8.2 0.0 copy-start.3
  8.2 0.9 copy-done.3
  9.1 0.0 copy-start.4
  9.1 0.9 copy-done.4
  10.1 0.0 copy-start.5
  10.1 0.7 copy-done.5
  10.8 0.0 copy-start.6
  10.8 0.0 copy-start.7
  10.8 2.5 %local_part.1 = (bf16[16,80,128]{2,1,0:T(8,128)(2,1)}, f32[8,128,128]{2,1,0:T(8,128)S(1)}, bf16[8,128,128]{2,1,0:T(8,128)(2,1)S(1)}, f32[128,128]{1,0:T(8,128)S(1)}) custom-call(bf16[1024,128]{1,0:T(8,128)(2,1)S(1)} %bitcast.22, bf16[1024,128]{1,0:T(8,128)(2,1)S(1)} %bitcast.23, bf16[1024,128]{1,0:T(8,128)(2,1)S(1)} %bitcast.24, f32[8,128]{1,0:T(8,128)S(1)} %copy-done.5), custom_call_target="tpu_custom_call" | custom-call | flops 134217728 | bytes 2097152 | tf_op jit(solution)/shard_map/local_part/pallas_call | solution.py:215
  13.2 15.7 %all-to-all-start = ((bf16[16,80,128]{2,1,0:T(8,128)(2,1)}), bf16[16,80,128]{2,1,0:T(8,128)(2,1)S(1)}, u32[]{:S(2)}, u32[]{:S(2)}) async-start(bf16[16,80,128]{2,1,0:T(8,128)(2,1)} %get-tuple-element.15), calls=%async_computation | async-start | bytes 655360 | tf_op jit(solution)/shard_map/all_to_all | solution.py:230
  29.0 0.0 all-gather.3.cloned.1.call-start
  29.0 0.0 copy-done.6
  29.1 0.0 copy-done.7
  29.1 0.6 pad_maximum_fusion
  29.7 0.0 all-gather.3.cloned.1.call-update
  29.7 14.5 %all-to-all-done.got_ref = bf16[16,80,128]{2,1,0:T(8,128)(2,1)S(1)} async-done(((bf16[16,80,128]{2,1,0:T(8,128)(2,1)}), bf16[16,80,128]{2,1,0:T(8,128)(2,1)S(1)}, u32[]{:S(2)}, u32[]{:S(2)}) %all-to-all-start) | async-done | bytes 327712 | tf_op jit(solution)/shard_map/all_to_all | solution.py:230
  44.2 0.0 copy-done
  44.2 1.2 row_scan.1
  45.4 4.2 %all-to-all-start.1 = ((bf16[4,1104,128]{2,1,0:T(8,128)(2,1)}), bf16[4,1104,128]{2,1,0:T(8,128)(2,1)S(1)}, u32[]{:S(2)}, u32[]{:S(2)}) async-start(bf16[4,1104,128]{2,1,0:T(8,128)(2,1)} %get-tuple-element.16), calls=%async_computation.1 | async-start | bytes 2260992 | tf_op jit(solution)/shard_map/all_to_all | solution.py:245
  49.6 0.1 pad_add_fusion.pos_ref
  49.7 10.1 %all-to-all-done.1.got_ref = bf16[4,1104,128]{2,1,0:T(8,128)(2,1)S(1)} async-done(((bf16[4,1104,128]{2,1,0:T(8,128)(2,1)}), bf16[4,1104,128]{2,1,0:T(8,128)(2,1)S(1)}, u32[]{:S(2)}, u32[]{:S(2)}) %all-to-all-start.1) | async-done | bytes 1130528 | tf_op jit(solution)/shard_map/all_to_all | solution.py:245
  59.8 0.6 carry_in.1
  60.4 29.4 %all_to_all.20 = bf16[16,64,128]{2,1,0:T(8,128)(2,1)S(1)} all-to-all(bf16[16,64,128]{2,1,0:T(8,128)(2,1)S(1)} %carry_in.1), channel_id=1, replica_groups={{0,8,16,24,32,40,48,56,64,72,80,88,96,104,112,120},{128,136,144,152,160..., dimensions={0} | all-to-all | bytes 524288 | tf_op jit(solution)/shard_map/all_to_all | solution.py:262
  89.9 0.3 mix.1
  90.2 9.2 %all-gather.3.cloned.1.call-done = bf16[4096,128]{1,0:T(8,128)(2,1)} async-done(((bf16[256,128]{1,0:T(8,128)(2,1)}), bf16[4096,128]{1,0:T(8,128)(2,1)}) %all-gather.3.cloned.1.call-update) | async-done | bytes 1048592 | tf_op jit(solution)/shard_map/all_gather | solution.py:212
  99.4 0.0 copy-start.1
  99.4 1.2 copy-done.1
  100.7 24.9 %attend.1 = bf16[4,1056,128]{2,1,0:T(8,128)(2,1)} custom-call(s32[2]{0:T(128)S(1)} %pad_add_fusion.pos_ref, bf16[4,1104,128]{2,1,0:T(8,128)(2,1)S(1)} %all-to-all-done.1.got_ref, bf16[16,256,128]{2,1,0:T(8,128)(2,1)S(1)} %bitcast.21), custom_call_target="tpu_custom_call" | custom-call | flops 6442450944 | bytes 4194304 | tf_op jit(solution)/shard_map/attend/pallas_call | solution.py:279
  125.6 0.0 copy-start.8
  125.6 3.6 %all-to-all-start.3 = ((bf16[4,1056,128]{2,1,0:T(8,128)(2,1)}), bf16[4,1056,128]{2,1,0:T(8,128)(2,1)S(1)}, u32[]{:S(2)}, u32[]{:S(2)}) async-start(bf16[4,1056,128]{2,1,0:T(8,128)(2,1)} %attend.1), calls=%async_computation.3 | async-start | bytes 2162688 | tf_op jit(solution)/shard_map/all_to_all | solution.py:293
  129.2 22.8 %psum.7 = f32[1,128]{1,0:T(1,128)S(1)} all-reduce(f32[1,128]{1,0:T(1,128)S(1)} %get-tuple-element.20), channel_id=1, replica_groups=mesh['ctx'=64,'head'=8] {'head'}, use_global_device_ids=true, to_apply=%region_0.1 | all-reduce | flops 128 | bytes 1024 | tf_op jit(solution)/shard_map/psum | solution.py:273
  152.0 0.0 copy-done.8
  152.0 0.9 fusion.1
  152.9 0.0 all-to-all-done.3.got_ref
  152.9 1.3 merge.1
  (1 shorter events, 0.0 us)
Async XLA Ops:
  7.2 37.1 %copy-start = (bf16[128,8,128]{2,1,0:T(8,128)(2,1)S(1)}, bf16[128,8,128]{2,1,0:T(8,128)(2,1)}, u32[]{:S(2)}) copy-start(bf16[128,8,128]{2,1,0:T(8,128)(2,1)} %param.13) | copy-start | bytes 786436
  7.2 1.0 copy-start.2
  8.2 0.9 copy-start.3
  9.1 0.9 copy-start.4
  10.1 0.7 copy-start.5
  10.8 18.3 %copy-start.6 = (bf16[128,1,128]{2,0,1:T(8,128)(2,1)S(1)}, bf16[128,1,128]{2,0,1:T(8,128)(2,1)}, u32[]{:S(2)}) copy-start(bf16[128,1,128]{2,0,1:T(8,128)(2,1)} %param.15) | copy-start | bytes 98308
  10.8 18.3 %copy-start.7 = (bf16[128,1,128]{2,0,1:T(8,128)(2,1)S(1)}, bf16[128,1,128]{2,0,1:T(8,128)(2,1)}, u32[]{:S(2)}) copy-start(bf16[128,1,128]{2,0,1:T(8,128)(2,1)} %param.14) | copy-start | bytes 98308
  13.2 31.0 %all-to-all-start = ((bf16[16,80,128]{2,1,0:T(8,128)(2,1)}), bf16[16,80,128]{2,1,0:T(8,128)(2,1)S(1)}, u32[]{:S(2)}, u32[]{:S(2)}) async-start(bf16[16,80,128]{2,1,0:T(8,128)(2,1)} %get-tuple-element.15), calls=%async_computation | async-start | bytes 655360 | tf_op jit(solution)/shard_map/all_to_all | solution.py:230
  29.0 70.4 %all-gather.3.cloned.1.call-start = ((), (), s32[]{:S(2)}) async-start(), calls=%async_computation.4 | async-start | bytes 1114112 | tf_op jit(solution)/shard_map/all_gather | solution.py:212
  45.4 14.4 %all-to-all-start.1 = ((bf16[4,1104,128]{2,1,0:T(8,128)(2,1)}), bf16[4,1104,128]{2,1,0:T(8,128)(2,1)S(1)}, u32[]{:S(2)}, u32[]{:S(2)}) async-start(bf16[4,1104,128]{2,1,0:T(8,128)(2,1)} %get-tuple-element.16), calls=%async_computation.1 | async-start | bytes 2260992 | tf_op jit(solution)/shard_map/all_to_all | solution.py:245
  99.4 1.2 copy-start.1
  125.6 26.4 %copy-start.8 = (f32[8,128]{1,0:T(8,128)S(1)}, f32[8,128]{1,0:T(8,128)}, u32[]{:S(2)}) copy-start(f32[8,128]{1,0:T(8,128)} %param.12) | copy-start | bytes 12292
  125.6 27.3 %all-to-all-start.3 = ((bf16[4,1056,128]{2,1,0:T(8,128)(2,1)}), bf16[4,1056,128]{2,1,0:T(8,128)(2,1)S(1)}, u32[]{:S(2)}, u32[]{:S(2)}) async-start(bf16[4,1056,128]{2,1,0:T(8,128)(2,1)} %attend.1), calls=%async_computation.3 | async-start | bytes 2162688 | tf_op jit(solution)/shard_map/all_to_all | solution.py:293
Sparse Core Ops, SparseCore 0:
  32.5 66.9 all-gather.2

commit v2 on v1

v2 whole, which is shorter than its diff:
```python
import jax
import jax.numpy as jnp
from jax import lax
from jax.experimental import pallas as pl
from jax.experimental.pallas import tpu as pltpu
from jax.sharding import PartitionSpec as P

QUERY_HEADS = 64
HD = 128
TOK = 128
HEADS = 8
ROWS = TOK * HEADS
Y, Z = 4, 16
SLICE = ROWS // Z
STATE_ROWS = SLICE + 16
STAT_ROWS = 32
SPARE = 96
KV_ROWS = 2 * TOK + SPARE
LOG2E = 1.4426950408889634
SCALE2 = LOG2E * HD ** (-0.5)
NEG = -1e30
F32, BF16 = jnp.float32, jnp.bfloat16
Z_GROUPS = [[y * Z + z for z in range(Z)] for y in range(Y)]
PAIR_GROUPS = [[y * Z + 2 * p, y * Z + 2 * p + 1] for y in range(Y) for p in range(Z // 2)]
SPREAD_GROUPS = [[y * Z + 2 * p + odd for p in range(Z // 2)] for y in range(Y) for odd in range(2)]
Y_GROUPS = [[y * Z + z for y in range(Y)] for z in range(Z)]


def split3(x):
    high = x.astype(BF16)
    rest = x - high.astype(F32)
    mid = rest.astype(BF16)
    low = (rest - mid.astype(F32)).astype(BF16)
    return high, mid, low


def scalar_rows(x):
    high, mid, low = (part.astype(F32) for part in split3(x))
    row = lax.broadcasted_iota(jnp.int32, (16, 128), 0)
    out = jnp.where(row == 0, high, jnp.where(row == 1, mid, jnp.where(row == 2, low, 0.0)))
    return out.astype(BF16)


def scalar_back(rows):
    rows = rows.astype(F32)
    return rows[0:1] + rows[1:2] + rows[2:3]


def silu(ref):
    x = ref[...].astype(F32)
    return x / (1.0 + jnp.exp(-x))


def local_kernel(
    q_hbm, k_hbm, v_hbm, decay_hbm, pay_ref, inner_ref, act_ref, ecum_ref,
    q_ref, k_ref, v_ref, decay_ref, sq, sk, sv, sems,
):
    pairs = ((decay_hbm, decay_ref), (k_hbm, k_ref), (v_hbm, v_ref), (q_hbm, q_ref))
    copies = [pltpu.make_async_copy(a, b, sems.at[i]) for i, (a, b) in enumerate(pairs)]
    for copy in copies:
        copy.start()
    copies[0].wait()
    lane = lax.broadcasted_iota(jnp.int32, (HEADS, TOK), 1)
    cum = decay_ref[...]
    step = 1
    while step < TOK:
        cum = cum + jnp.where(lane >= step, pltpu.roll(cum, step, 1), 0.0)
        step *= 2
    cum_col = jnp.transpose(jnp.concatenate([cum] * (TOK // HEADS), axis=0))
    ecum_ref[...] = jnp.exp(cum_col)
    causal = lax.broadcasted_iota(jnp.int32, (TOK, TOK), 0) >= lax.broadcasted_iota(
        jnp.int32, (TOK, TOK), 1
    )
    copies[1].wait()
    sk[...] = silu(k_ref)
    copies[2].wait()
    sv[...] = silu(v_ref)
    copies[3].wait()
    sq[...] = silu(q_ref)
    for h in range(HEADS):
        mine = pl.ds(h, TOK, stride=HEADS)
        aq = sq[mine, :].astype(BF16)
        ak = sk[mine, :].astype(BF16)
        av = sv[mine, :].astype(BF16)
        act_ref[h] = aq
        row = cum[h : h + 1, :]
        col = cum_col[:, h : h + 1]
        last = row[:, TOK - 1 : TOK]
        scores = lax.dot_general(aq, ak, (((1,), (1,)), ((), ())), preferred_element_type=F32)
        weights = (scores * jnp.exp(jnp.where(causal, col - row, NEG))).astype(BF16)
        inner_ref[h] = jnp.dot(weights, av, preferred_element_type=F32)
        scaled = (ak.astype(F32) * jnp.exp(last - col)).astype(BF16)
        state = lax.dot_general(scaled, av, (((0,), (0,)), ((), ())), preferred_element_type=F32)
        extra = scalar_rows(jnp.broadcast_to(last, (1, 128)))
        for half in range(2):
            pay_ref[2 * h + half, 0:SLICE, :] = state[half * SLICE : (half + 1) * SLICE].astype(BF16)
            pay_ref[2 * h + half, SLICE:STATE_ROWS, :] = extra


def keep_kernel(pay_in, inner_ref, act_ref, ecum_ref, pay_out):
    pass


def row_kernel(got_ref, q_ref, pay_ref):
    run = jnp.zeros((SLICE, 128), F32)
    total = jnp.zeros((1, 128), F32)
    for z in range(Z):
        decay = scalar_back(got_ref[z, SLICE:STATE_ROWS, :])
        run = run * jnp.exp(decay) + got_ref[z, 0:SLICE, :].astype(F32)
        total = total + decay
    extra = scalar_rows(total)
    for y in range(Y):
        pay_ref[y, 0:SLICE, :] = run.astype(BF16)
        pay_ref[y, SLICE:STATE_ROWS, :] = extra
        pay_ref[y, STATE_ROWS:, :] = q_ref[...]


def carry_kernel(pos_ref, rows_ref, got_ref, out_ref):
    mine = pos_ref[0]
    run = jnp.zeros((SLICE, 128), F32)
    for y in range(Y - 1):
        decay = scalar_back(rows_ref[y, SLICE:STATE_ROWS, :])
        new = run * jnp.exp(decay) + rows_ref[y, 0:SLICE, :].astype(F32)
        run = jnp.where(y < mine, new, run)
    for z in range(Z):
        out_ref[z] = run.astype(BF16)
        decay = scalar_back(got_ref[z, SLICE:STATE_ROWS, :])
        run = run * jnp.exp(decay) + got_ref[z, 0:SLICE, :].astype(F32)


def mix_kernel(act_ref, inner_ref, ecum_ref, prior_ref, mixed_ref, square_ref):
    squares = jnp.zeros((TOK, HD), F32)
    for h in range(HEADS):
        outer = jnp.dot(act_ref[h], prior_ref[h * HD : (h + 1) * HD, :], preferred_element_type=F32)
        mixed = inner_ref[h] + outer * ecum_ref[:, h : h + 1]
        squares = squares + mixed * mixed
        mixed_ref[pl.ds(h, TOK, stride=HEADS), :] = mixed
    square_ref[...] = jnp.broadcast_to(jnp.sum(jnp.transpose(squares), axis=0, keepdims=True), (8, TOK))


QT = 512
CHUNK = 256
KEYS = Z * TOK


def attend_kernel(pos_ref, q_ref, kv_hbm, out_ref, keys, vaug, s_even, s_odd, stats, sems):
    my_y, my_z = pos_ref[0], pos_ref[1]
    get_keys = pltpu.make_async_copy(kv_hbm.at[:, 0:TOK, :], keys, sems.at[0])
    get_values = pltpu.make_async_copy(kv_hbm.at[:, TOK : 2 * TOK, :], vaug.at[:, :, 0:HD], sems.at[1])
    get_keys.start()
    get_values.start()
    vaug[:, :, HD:] = jnp.ones((Z, TOK, HD), BF16)
    get_keys.wait()
    get_values.wait()
    held = (s_even, s_odd)
    tiles, chunks, blocks = ROWS // QT, KEYS // CHUNK, CHUNK // TOK

    def score(y, i, j, top, masked):
        q = q_ref[y, STATE_ROWS + i * QT : STATE_ROWS + (i + 1) * QT, :]
        part = keys[j * blocks : (j + 1) * blocks].reshape(CHUNK, HD)
        s = lax.dot_general(q, part, (((1,), (1,)), ((), ())), preferred_element_type=F32)
        if masked:
            row = lax.broadcasted_iota(jnp.int32, (QT, CHUNK), 0)
            key = lax.broadcasted_iota(jnp.int32, (QT, CHUNK), 1)
            pos = my_z * TOK - j * CHUNK + (row + i * QT) // HEADS
            s = jnp.where(pos >= key, s, NEG)
        held[i % 2][:, j * CHUNK : (j + 1) * CHUNK] = s
        for lanes in range(blocks):
            new = s[:, lanes * 128 : (lanes + 1) * 128]
            top = new if top is None else jnp.maximum(top, new)
        return top

    def unit(y, masked):
        top = None
        for j in range(chunks):
            top = score(y, 0, j, top, masked)
        for i in range(tiles):
            shift = jnp.max(top, axis=1, keepdims=True) * SCALE2
            top = acc = None
            for j in range(chunks):
                if i + 1 < tiles:
                    top = score(y, i + 1, j, top, masked)
                s = held[i % 2][:, j * CHUNK : (j + 1) * CHUNK]
                p = jnp.exp2(s * SCALE2 - shift).astype(BF16)
                part = vaug[j * blocks : (j + 1) * blocks].reshape(CHUNK, 2 * HD)
                new = jnp.dot(p, part, preferred_element_type=F32)
                acc = new if acc is None else acc + new
            total = acc[:, HD:]
            out_ref[y, STAT_ROWS + i * QT : STAT_ROWS + (i + 1) * QT, :] = (acc[:, :HD] / total).astype(BF16)
            lse = shift + jnp.log(total) * LOG2E
            for b in range(QT // 128):
                at = i * (QT // 128) + b
                stats[at : at + 1, :] = jnp.transpose(lse[b * 128 : (b + 1) * 128])[0:1]
        high, mid, low = split3(stats[...])
        zero = jnp.zeros((HEADS, 128), BF16)
        out_ref[y, 0:16, :] = jnp.concatenate([high, mid], axis=0)
        out_ref[y, 16:32, :] = jnp.concatenate([low, zero], axis=0)

    def skip(y, carry):
        out_ref[y, 0:16, :] = jnp.concatenate([jnp.full((8, 128), NEG, BF16), jnp.zeros((8, 128), BF16)], axis=0)
        out_ref[y, 16:, :] = jnp.zeros((ROWS + 16, HD), BF16)
        return carry

    def other(y, carry):
        unit(y, False)
        return carry

    lax.fori_loop(0, my_y, skip, 0)
    unit(my_y, True)
    lax.fori_loop(my_y + 1, Y, other, 0)


def merge_kernel(got_ref, out_ref):
    lse = []
    for y in range(Y):
        first = got_ref[y, 0:16, :].astype(F32)
        second = got_ref[y, 16:32, :].astype(F32)
        lse.append(first[0:8] + first[8:16] + second[0:8])
    top = jnp.maximum(jnp.maximum(lse[0], lse[1]), jnp.maximum(lse[2], lse[3]))
    w = [jnp.exp2(x - top) for x in lse]
    total = w[0] + w[1] + w[2] + w[3]
    w = [x / total for x in w]
    for b in range(ROWS // 128):
        rows = slice(STAT_ROWS + b * 128, STAT_ROWS + (b + 1) * 128)
        acc = jnp.zeros((128, HD), F32)
        for y in range(Y):
            col = jnp.transpose(jnp.broadcast_to(w[y][b : b + 1, :], (128, 128)))
            acc = acc + col * got_ref[y, rows, :].astype(F32)
        out_ref[b * 128 : (b + 1) * 128, :] = acc.astype(BF16)


def shape(*dims, kind=BF16):
    return jax.ShapeDtypeStruct(dims, kind)


VM = pl.BlockSpec(memory_space=pltpu.VMEM)
SM = pl.BlockSpec(memory_space=pltpu.SMEM)
HB = pl.BlockSpec(memory_space=pltpu.HBM)
ANY = pl.BlockSpec(memory_space=pl.ANY)


def params(mib=16):
    return pltpu.CompilerParams(vmem_limit_bytes=mib << 20)


def cost(flops, nbytes, exps=0):
    return pl.CostEstimate(flops=flops, bytes_accessed=nbytes, transcendentals=exps)


def local(lin_query, lin_key, lin_value, log_decay, norm_gain, attn_query, attn_key, attn_value):
    index = lax.axis_index("ctx")
    pos = jnp.stack([lax.shift_right_logical(index, 4), index & (Z - 1)]).astype(jnp.int32)

    flat = lambda x: x.reshape(ROWS, HD)
    kv = [attn_key.reshape(TOK, HD), attn_value.reshape(TOK, HD), jnp.zeros((SPARE, HD), BF16)]
    kv = jnp.concatenate(kv, axis=0)
    kv = lax.all_gather(kv, "ctx", axis_index_groups=PAIR_GROUPS)
    kv, pos, lin_query, lin_key, lin_value = lax.optimization_barrier(
        (kv, pos, lin_query, lin_key, lin_value)
    )
    kv_row = lax.all_gather(kv, "ctx", axis_index_groups=SPREAD_GROUPS).reshape(Z, KV_ROWS, HD)
    pay, inner, act, ecum = pl.pallas_call(
        local_kernel,
        out_shape=(
            shape(Z, STATE_ROWS, 128),
            shape(HEADS, TOK, HD, kind=F32),
            shape(HEADS, TOK, HD),
            shape(TOK, 128, kind=F32),
        ),
        in_specs=[ANY] * 4,
        out_specs=(VM,) * 4,
        scratch_shapes=[pltpu.VMEM((ROWS, HD), BF16)] * 3
        + [pltpu.VMEM((HEADS, TOK), F32)]
        + [pltpu.VMEM((ROWS, HD), F32)] * 3
        + [pltpu.SemaphoreType.DMA((4,))],
        compiler_params=params(62),
        cost_estimate=cost(1, 1),
        name="local_part",
    )(flat(lin_query), flat(lin_key), flat(lin_value), log_decay)
    pay = pl.pallas_call(
        keep_kernel,
        out_shape=shape(Z, STATE_ROWS, 128),
        in_specs=[ANY] * 4,
        out_specs=ANY,
        input_output_aliases={0: 0},
        compiler_params=params(62),
        cost_estimate=cost(1, 1),
        name="keep",
    )(pay, inner, act, ecum)
    got = lax.all_to_all(pay, "ctx", 0, 0, axis_index_groups=Z_GROUPS)
    got, query = lax.optimization_barrier((got, flat(attn_query)))

    pay = pl.pallas_call(
        row_kernel,
        out_shape=shape(Y, STATE_ROWS + ROWS, 128),
        in_specs=[VM, VM],
        out_specs=VM,
        compiler_params=params(),
        cost_estimate=cost(1, 1),
        name="row_scan",
    )(got, query)
    queries = lax.all_to_all(pay, "ctx", 0, 0, axis_index_groups=Y_GROUPS)

    pay = pl.pallas_call(
        carry_kernel,
        out_shape=shape(Z, SLICE, 128),
        grid=(1,),
        in_specs=[
            SM,
            pl.BlockSpec((Y, STATE_ROWS, 128), lambda i: (0, 0, 0)),
            pl.BlockSpec((Z, STATE_ROWS, 128), lambda i: (0, 0, 0)),
        ],
        out_specs=pl.BlockSpec((Z, SLICE, 128), lambda i: (0, 0, 0)),
        compiler_params=params(),
        cost_estimate=cost(1, 1),
        name="carry_in",
    )(pos, queries, got)
    pay, queries = lax.optimization_barrier((pay, queries))
    prior = lax.all_to_all(pay, "ctx", 0, 0, axis_index_groups=Z_GROUPS)

    pay = pl.pallas_call(
        attend_kernel,
        out_shape=shape(Y, STAT_ROWS + ROWS, HD),
        in_specs=[SM, VM, HB],
        out_specs=VM,
        scratch_shapes=[
            pltpu.VMEM((Z, TOK, HD), BF16),
            pltpu.VMEM((Z, TOK, 2 * HD), BF16),
            pltpu.VMEM((QT, KEYS), F32),
            pltpu.VMEM((QT, KEYS), F32),
            pltpu.VMEM((HEADS, 128), F32),
            pltpu.SemaphoreType.DMA((2,)),
        ],
        compiler_params=params(62),
        cost_estimate=cost(3 * 2 * 4 * ROWS * KEYS * HD, 4 << 20, 4 * ROWS * KEYS),
        name="attend",
    )(pos, queries, kv_row)
    pay, prior = lax.optimization_barrier((pay, prior))
    got = lax.all_to_all(pay, "ctx", 0, 0, axis_index_groups=Y_GROUPS)

    mixed, squares = pl.pallas_call(
        mix_kernel,
        out_shape=(shape(ROWS, HD, kind=F32), shape(8, TOK, kind=F32)),
        in_specs=[VM] * 4,
        out_specs=(VM,) * 2,
        compiler_params=params(),
        cost_estimate=cost(2 * 8 * 128**3, 2 << 20),
        name="mix",
    )(act, inner, ecum, prior.reshape(ROWS, HD))

    total = jnp.sum(lax.all_gather(squares, "head")[:, 0], axis=0)
    inverse = lax.rsqrt(total / (QUERY_HEADS * HD) + 1e-06)
    lin_out = mixed.reshape(TOK, HEADS, HD) * inverse[:, None, None] * norm_gain[None]
    lin_out = lin_out.astype(BF16)

    attn_out = pl.pallas_call(
        merge_kernel,
        out_shape=shape(ROWS, HD),
        in_specs=[VM],
        out_specs=VM,
        compiler_params=params(),
        cost_estimate=cost(1 << 20, 2 << 20),
        name="merge",
    )(got)
    return lin_out, attn_out.reshape(TOK, HEADS, HD)


def solution(mesh):
    act = P("ctx", "head", None)
    return jax.shard_map(
        local,
        mesh=mesh,
        in_specs=(act, act, act, P("head", "ctx"), P("head", None), act, act, act),
        out_specs=(act, act),
        check_vma=False,
    )
```

time: 162 us -> 128 us (0.79)
  waiting for transfers between devices: 33.9 us -> 2.66 us
  blocking collectives: 52.2 us -> 64.7 us
  Pallas kernels: 30.9 us -> 21.9 us
  local copies, waits for them, and re-layouts: 4.81 us -> 0.05 us
  starting transfers between devices: 23.6 us -> 21.7 us
    psum x1 -> x0, blocking collectives: 22.8 us -> none  [local(): total = lax.psum(squares, 'head')]
    all_gather x0 -> x2, blocking collectives: none -> 20.3 us  [the longest x1 15.2 us: local(): total = jnp.sum(lax.all_gather(squares, 'head')[:, 0], axis=0)]
    all_to_all x1 -> x2, blocking collectives: 29.4 us -> 44.4 us  [the longest x1 30.2 us: local(): got = lax.all_to_all(pay, 'ctx', 0, 0, axis_index_groups=Z_GROUPS)]
    all_to_all x1, waiting for transfers between devices: 14.5 us -> 0.01 us  [local(): prior = lax.all_to_all(pay, 'ctx', 0, 0, axis_index_groups=Z_GROUPS)]
    all_to_all x2 -> x1, waiting for transfers between devices: 10.1 us -> 0.01 us  [local(): got = lax.all_to_all(pay, 'ctx', 0, 0, axis_index_groups=Y_GROUPS)]
    pallas_call x1, Pallas kernels: 24.9 us -> 14.8 us  [local(): pl.pallas_call(attend_kernel, out_shape=shape(Y, STAT_ROWS + ROWS, HD), i...]
    all_gather x1, waiting for transfers between devices: 9.25 us -> 2.64 us  [local(): lax.all_gather(kv, 'ctx', axis_index_groups=SPREAD_GROUPS)]
    unnamed x18 -> x14, local copies, waits for them, and re-layouts: 4.81 us -> 0.03 us
  transfers between devices with their start and end apart: 4 -> 3, of which waited for: 3 -> 1; matrix products, arithmetic and copies ran while one was open for 1% -> 1% of each run, Pallas kernels for 1% -> 16%
where the time goes in v2:
time: 128 us; the launch traced here: 127 us
  blocking collectives  64.7 us (51%)
  Pallas kernels  21.9 us (17%)
  starting transfers between devices  21.7 us (17%)
  between operations  14.2 us (11%)
  waiting for transfers between devices  2.66 us (2%)
  other arithmetic  1.91 us (1%)
    all_to_all x1, blocking collectives, local(): got = lax.all_to_all(pay, 'ctx', 0, 0, axis_index_groups=Z_GROUPS)  30.2 us
    all_to_all x1, starting transfers between devices, local(): prior = lax.all_to_all(pay, 'ctx', 0, 0, axis_index_groups=Z_GROUPS)  18 us
    all_gather x1, blocking collectives, local(): total = jnp.sum(lax.all_gather(squares, 'head')[:, 0], axis=0)  15.2 us
    pallas_call x1, Pallas kernels, local(): pl.pallas_call(attend_kernel, out_shape=shape(Y, STAT_ROWS + ROWS, HD), i...  14.8 us
    all_to_all x1, blocking collectives, local(): queries = lax.all_to_all(pay, 'ctx', 0, 0, axis_index_groups=Y_GROUPS)  14.2 us
    all_gather x1, blocking collectives, local(): kv = lax.all_gather(kv, 'ctx', axis_index_groups=PAIR_GROUPS)  5.14 us
    pallas_call x1, Pallas kernels, local(): pl.pallas_call(local_kernel, out_shape=(shape(Z, STATE_ROWS, 128), shape(...  3.9 us
    all_to_all x1, starting transfers between devices, local(): got = lax.all_to_all(pay, 'ctx', 0, 0, axis_index_groups=Y_GROUPS)  3.66 us
  transfers between devices with their start and end apart: 3, of which 1 were waited for; matrix products, arithmetic and copies ran while one was open for 1% of the time, Pallas kernels for 16%

profile of v2, /device:TPU:1, one launch (start us, length us, event | category | flops | bytes accessed | tf_op | source)
XLA Modules:
  0.0 127.1 jit_solution(632847116261476532)
XLA Ops:
  7.2 0.0 all-gather.5.cloned.1.call-start
  7.2 0.9 maximum_maximum_fusion
  8.1 5.1 %all-gather = bf16[704,128]{1,0:T(8,128)(2,1)} all-gather(bf16[352,128]{1,0:T(8,128)(2,1)S(1)} %maximum_maximum_fusion), channel_id=2, replica_groups={{0,8},{16,24},{32,40},{48,56},{64,72},{80,88},{96,104},{112,120},{128,1..., dimensions={0}, use_global_device_ids=true | all-gather | bytes 270336 | tf_op jit(solution)/shard_map/all_gather | solution.py:257
  13.3 0.1 pad_add_fusion.pos_ref
  13.4 0.0 copy-start.5
  13.4 0.0 all-gather.5.cloned.1.call-update
  13.4 3.9 %local_part.1 = (bf16[16,80,128]{2,1,0:T(8,128)(2,1)}, f32[8,128,128]{2,1,0:T(8,128)}, bf16[8,128,128]{2,1,0:T(8,128)(2,1)}, f32[128,128]{1,0:T(8,128)}) custom-call(bf16[1024,128]{1,0:T(8,128)(2,1)} %bitcast.21, bf16[1024,128]{1,0:T(8,128)(2,1)} %bitcast.22, bf16[1024,128]{1,0:T(8,128)(2,1)} %bitcast.23, f32[8,128]{1,0:T(8,128)} %decay_hbm.1), custom_call_target="tpu_custom_call" | custom-call | flops 1 | bytes 1 | tf_op jit(solution)/shard_map/local_part/pallas_call | solution.py:262
  17.3 0.0 copy-start.4
  17.3 30.2 %all_to_all.20.got_ref = bf16[16,80,128]{2,1,0:T(8,128)(2,1)S(1)} all-to-all(bf16[16,80,128]{2,1,0:T(8,128)(2,1)} %keep.1), channel_id=1, replica_groups={{0,8,16,24,32,40,48,56,64,72,80,88,96,104,112,120},{128,136,144,152,160..., dimensions={0} | all-to-all | bytes 655360 | tf_op jit(solution)/shard_map/all_to_all | solution.py:290
  47.5 0.0 copy-done.4
  47.5 0.2 row_scan.1
  47.7 14.2 %all_to_all.21.rows_ref.q_ref = bf16[4,1104,128]{2,1,0:T(8,128)(2,1)S(1)} all-to-all(bf16[4,1104,128]{2,1,0:T(8,128)(2,1)S(1)} %row_scan.1), channel_id=1, replica_groups={{0,128,256,384},{8,136,264,392},{16,144,272,400},{24,152,280,408},{32,1..., dimensions={0} | all-to-all | bytes 2260992 | tf_op jit(solution)/shard_map/all_to_all | solution.py:302
  61.8 0.0 copy-done.5
  61.8 0.0 copy-start
  61.8 1.3 %carry_in.1 = bf16[16,64,128]{2,1,0:T(8,128)(2,1)} custom-call(s32[2]{0:T(128)S(1)} %pad_add_fusion.pos_ref, bf16[4,1104,128]{2,1,0:T(8,128)(2,1)S(1)} %all_to_all.21.rows_ref.q_ref, bf16[16,80,128]{2,1,0:T(8,128)(2,1)S(1)} %all_to_all.20.got_ref), custom_call_target="tpu_custom_call" | custom-call | flops 1 | bytes 1 | tf_op jit(solution)/shard_map/carry_in/pallas_call | solution.py:304
  63.2 18.0 %all-to-all-start.2 = ((bf16[16,64,128]{2,1,0:T(8,128)(2,1)}), bf16[16,64,128]{2,1,0:T(8,128)(2,1)S(1)}, u32[]{:S(2)}, u32[]{:S(2)}) async-start(bf16[16,64,128]{2,1,0:T(8,128)(2,1)} %carry_in.1), calls=%async_computation.2 | async-start | bytes 524288 | tf_op jit(solution)/shard_map/all_to_all | solution.py:319
  81.2 2.6 %all-gather.5.cloned.1.call-done.kv_hbm = bf16[16,352,128]{2,1,0:T(8,128)(2,1)} async-done(((bf16[2,352,128]{2,1,0:T(8,128)(2,1)}), bf16[16,352,128]{2,1,0:T(8,128)(2,1)}) %all-gather.5.cloned.1.call-update) | async-done | bytes 1441808 | tf_op jit(solution)/shard_map/all_gather | solution.py:261
  83.8 0.0 copy-done
  83.8 14.8 %attend.1 = bf16[4,1056,128]{2,1,0:T(8,128)(2,1)} custom-call(s32[2]{0:T(128)} %copy-done.5, bf16[4,1104,128]{2,1,0:T(8,128)(2,1)} %copy-done, bf16[16,352,128]{2,1,0:T(8,128)(2,1)} %all-gather.5.cloned.1.call-done.kv_hbm), custom_call_target="tpu_custom_call" | custom-call | flops 6442450944 | bytes 4194304 | tf_op jit(solution)/shard_map/attend/pallas_call | solution.py:321
  98.7 0.0 copy-start.1
  98.7 0.0 copy-start.2
  98.7 0.0 copy-start.3
  98.7 0.0 copy-start.6
  98.7 0.0 all-to-all-done.2
  98.7 3.7 %all-to-all-start.3 = ((bf16[4,1056,128]{2,1,0:T(8,128)(2,1)}), bf16[4,1056,128]{2,1,0:T(8,128)(2,1)S(1)}, u32[]{:S(2)}, u32[]{:S(2)}) async-start(bf16[4,1056,128]{2,1,0:T(8,128)(2,1)} %attend.1), calls=%async_computation.3 | async-start | bytes 2162688 | tf_op jit(solution)/shard_map/all_to_all | solution.py:339
  102.4 0.0 copy-done.1
  102.4 0.0 copy-done.2
  102.4 0.0 copy-done.3
  102.4 0.3 mix.1
  102.8 15.2 %all-gather.2 = f32[64,128]{1,0:T(8,128)S(1)} all-gather(f32[8,128]{1,0:T(8,128)S(1)} %get-tuple-element.34), channel_id=4, replica_groups=mesh['ctx'=64,'head'=8] {'head'}, dimensions={0}, use_global_device_ids=true | all-gather | bytes 36864 | tf_op jit(solution)/shard_map/all_gather | solution.py:351
  118.0 0.0 copy-done.6
  118.0 0.9 fusion.1
  118.9 0.0 all-to-all-done.3.got_ref
  118.9 1.3 %merge.1 = bf16[1024,128]{1,0:T(8,128)(2,1)} custom-call(bf16[4,1056,128]{2,1,0:T(8,128)(2,1)S(1)} %all-to-all-done.3.got_ref), custom_call_target="tpu_custom_call" | custom-call | flops 1048576 | bytes 2097152 | tf_op jit(solution)/shard_map/merge/pallas_call | solution.py:356
  (5 shorter events, 0.0 us)
Async XLA Ops:
  7.2 76.7 %all-gather.5.cloned.1.call-start = ((), (), s32[]{:S(2)}) async-start(), calls=%async_computation.4 | async-start | bytes 1622016 | tf_op jit(solution)/shard_map/all_gather | solution.py:261
  13.4 48.5 %copy-start.5 = (s32[2]{0:T(128)}, s32[2]{0:T(128)S(1)}, u32[]{:S(2)}) copy-start(s32[2]{0:T(128)S(1)} %pad_add_fusion.pos_ref) | copy-start | bytes 28
  17.3 30.2 %copy-start.4 = (bf16[128,8,128]{2,1,0:T(8,128)(2,1)S(1)}, bf16[128,8,128]{2,1,0:T(8,128)(2,1)}, u32[]{:S(2)}) copy-start(bf16[128,8,128]{2,1,0:T(8,128)(2,1)} %param.13) | copy-start | bytes 786436
  61.8 22.0 %copy-start = (bf16[4,1104,128]{2,1,0:T(8,128)(2,1)}, bf16[4,1104,128]{2,1,0:T(8,128)(2,1)S(1)}, u32[]{:S(2)}) copy-start(bf16[4,1104,128]{2,1,0:T(8,128)(2,1)S(1)} %all_to_all.21.rows_ref.q_ref) | copy-start | bytes 3391492
  63.2 35.5 %all-to-all-start.2 = ((bf16[16,64,128]{2,1,0:T(8,128)(2,1)}), bf16[16,64,128]{2,1,0:T(8,128)(2,1)S(1)}, u32[]{:S(2)}, u32[]{:S(2)}) async-start(bf16[16,64,128]{2,1,0:T(8,128)(2,1)} %carry_in.1), calls=%async_computation.2 | async-start | bytes 524288 | tf_op jit(solution)/shard_map/all_to_all | solution.py:319
  98.7 3.7 %copy-start.1 = (f32[8,128,128]{2,1,0:T(8,128)S(1)}, f32[8,128,128]{2,1,0:T(8,128)}, u32[]{:S(2)}) copy-start(f32[8,128,128]{2,1,0:T(8,128)} %get-tuple-element.23.inner_ref) | copy-start | bytes 1572868
  98.7 3.7 %copy-start.2 = (bf16[8,128,128]{2,1,0:T(8,128)(2,1)S(1)}, bf16[8,128,128]{2,1,0:T(8,128)(2,1)}, u32[]{:S(2)}) copy-start(bf16[8,128,128]{2,1,0:T(8,128)(2,1)} %get-tuple-element.22.act_ref) | copy-start | bytes 786436
  98.7 3.7 %copy-start.3 = (f32[128,128]{1,0:T(8,128)S(1)}, f32[128,128]{1,0:T(8,128)}, u32[]{:S(2)}) copy-start(f32[128,128]{1,0:T(8,128)} %get-tuple-element.24.ecum_ref) | copy-start | bytes 196612
  98.7 19.3 %copy-start.6 = (f32[8,128]{1,0:T(8,128)S(1)}, f32[8,128]{1,0:T(8,128)}, u32[]{:S(2)}) copy-start(f32[8,128]{1,0:T(8,128)} %param.12) | copy-start | bytes 12292
  98.7 20.2 %all-to-all-start.3 = ((bf16[4,1056,128]{2,1,0:T(8,128)(2,1)}), bf16[4,1056,128]{2,1,0:T(8,128)(2,1)S(1)}, u32[]{:S(2)}, u32[]{:S(2)}) async-start(bf16[4,1056,128]{2,1,0:T(8,128)(2,1)} %attend.1), calls=%async_computation.3 | async-start | bytes 2162688 | tf_op jit(solution)/shard_map/all_to_all | solution.py:339
Sparse Core Ops, SparseCore 0:
  13.5 70.2 all-gather.4

commit v3 on v2

--- a/solution.py
+++ b/solution.py
@@ -14,7 +14,7 @@
 SLICE = ROWS // Z
 STATE_ROWS = SLICE + 16
 STAT_ROWS = 32
-SPARE = 96
+SPARE = 88
 KV_ROWS = 2 * TOK + SPARE
 LOG2E = 1.4426950408889634
 SCALE2 = LOG2E * HD ** (-0.5)
@@ -135,7 +135,7 @@
         mixed = inner_ref[h] + outer * ecum_ref[:, h : h + 1]
         squares = squares + mixed * mixed
         mixed_ref[pl.ds(h, TOK, stride=HEADS), :] = mixed
-    square_ref[...] = jnp.broadcast_to(jnp.sum(jnp.transpose(squares), axis=0, keepdims=True), (8, TOK))
+    square_ref[...] = jnp.sum(jnp.transpose(squares), axis=0, keepdims=True)
 
 
 QT = 512
@@ -340,7 +340,7 @@
 
     mixed, squares = pl.pallas_call(
         mix_kernel,
-        out_shape=(shape(ROWS, HD, kind=F32), shape(8, TOK, kind=F32)),
+        out_shape=(shape(ROWS, HD, kind=F32), shape(1, TOK, kind=F32)),
         in_specs=[VM] * 4,
         out_specs=(VM,) * 2,
         compiler_params=params(),
@@ -348,8 +348,8 @@
         name="mix",
     )(act, inner, ecum, prior.reshape(ROWS, HD))
 
-    total = jnp.sum(lax.all_gather(squares, "head")[:, 0], axis=0)
-    inverse = lax.rsqrt(total / (QUERY_HEADS * HD) + 1e-06)
+    total = lax.psum(squares, "head")
+    inverse = lax.rsqrt(total[0] / (QUERY_HEADS * HD) + 1e-06)
     lin_out = mixed.reshape(TOK, HEADS, HD) * inverse[:, None, None] * norm_gain[None]
     lin_out = lin_out.astype(BF16)
 

time: 128 us -> 128 us (level)
    psum x0 -> x1, blocking collectives: none -> 15.3 us  [local(): total = lax.psum(squares, 'head')]
    all_gather x1 -> x0, blocking collectives: 15.2 us -> none  [local(): total = jnp.sum(lax.all_gather(squares, 'head')[:, 0], axis=0)]
where the time goes in v3:
time: 128 us; the launch traced here: 127 us
  blocking collectives  64.7 us (51%)
  Pallas kernels  21.9 us (17%)
  starting transfers between devices  21.6 us (17%)
  between operations  14.2 us (11%)
  waiting for transfers between devices  2.87 us (2%)
  other arithmetic  1.88 us (1%)
    all_to_all x1, blocking collectives, local(): got = lax.all_to_all(pay, 'ctx', 0, 0, axis_index_groups=Z_GROUPS)  30.2 us
    all_to_all x1, starting transfers between devices, local(): prior = lax.all_to_all(pay, 'ctx', 0, 0, axis_index_groups=Z_GROUPS)  17.9 us
    psum x1, blocking collectives, local(): total = lax.psum(squares, 'head')  15.3 us
    pallas_call x1, Pallas kernels, local(): pl.pallas_call(attend_kernel, out_shape=shape(Y, STAT_ROWS + ROWS, HD), i...  14.8 us
    all_to_all x1, blocking collectives, local(): queries = lax.all_to_all(pay, 'ctx', 0, 0, axis_index_groups=Y_GROUPS)  14.2 us
    all_gather x1, blocking collectives, local(): kv = lax.all_gather(kv, 'ctx', axis_index_groups=PAIR_GROUPS)  5.12 us
    pallas_call x1, Pallas kernels, local(): pl.pallas_call(local_kernel, out_shape=(shape(Z, STATE_ROWS, 128), shape(...  3.9 us
    all_to_all x1, starting transfers between devices, local(): got = lax.all_to_all(pay, 'ctx', 0, 0, axis_index_groups=Y_GROUPS)  3.66 us
  transfers between devices with their start and end apart: 3, of which 1 were waited for; matrix products, arithmetic and copies ran while one was open for 1% of the time, Pallas kernels for 16%

profile of v3, /device:TPU:1, one launch (start us, length us, event | category | flops | bytes accessed | tf_op | source)
XLA Modules:
  0.0 127.2 jit_solution(8817584204158226200)
XLA Ops:
  7.2 0.0 all-gather.4.cloned.1.call-start
  7.2 0.9 maximum_maximum_fusion
  8.1 5.1 %all-gather = bf16[688,128]{1,0:T(8,128)(2,1)} all-gather(bf16[344,128]{1,0:T(8,128)(2,1)S(1)} %maximum_maximum_fusion), channel_id=2, replica_groups={{0,8},{16,24},{32,40},{48,56},{64,72},{80,88},{96,104},{112,120},{128,1..., dimensions={0}, use_global_device_ids=true | all-gather | bytes 264192 | tf_op jit(solution)/shard_map/all_gather | solution.py:257
  13.3 0.1 pad_add_fusion.pos_ref
  13.3 0.0 copy-start.5
  13.3 0.0 all-gather.4.cloned.1.call-update
  13.4 3.9 %local_part.1 = (bf16[16,80,128]{2,1,0:T(8,128)(2,1)}, f32[8,128,128]{2,1,0:T(8,128)}, bf16[8,128,128]{2,1,0:T(8,128)(2,1)}, f32[128,128]{1,0:T(8,128)}) custom-call(bf16[1024,128]{1,0:T(8,128)(2,1)} %bitcast.22, bf16[1024,128]{1,0:T(8,128)(2,1)} %bitcast.23, bf16[1024,128]{1,0:T(8,128)(2,1)} %bitcast.24, f32[8,128]{1,0:T(8,128)} %decay_hbm.1), custom_call_target="tpu_custom_call" | custom-call | flops 1 | bytes 1 | tf_op jit(solution)/shard_map/local_part/pallas_call | solution.py:262
  17.3 0.0 copy-start.4
  17.3 30.2 %all_to_all.20.got_ref = bf16[16,80,128]{2,1,0:T(8,128)(2,1)S(1)} all-to-all(bf16[16,80,128]{2,1,0:T(8,128)(2,1)} %keep.1), channel_id=1, replica_groups={{0,8,16,24,32,40,48,56,64,72,80,88,96,104,112,120},{128,136,144,152,160..., dimensions={0} | all-to-all | bytes 655360 | tf_op jit(solution)/shard_map/all_to_all | solution.py:290
  47.5 0.0 copy-done.4
  47.5 0.2 row_scan.1
  47.7 14.2 %all_to_all.21.rows_ref.q_ref = bf16[4,1104,128]{2,1,0:T(8,128)(2,1)S(1)} all-to-all(bf16[4,1104,128]{2,1,0:T(8,128)(2,1)S(1)} %row_scan.1), channel_id=1, replica_groups={{0,128,256,384},{8,136,264,392},{16,144,272,400},{24,152,280,408},{32,1..., dimensions={0} | all-to-all | bytes 2260992 | tf_op jit(solution)/shard_map/all_to_all | solution.py:302
  61.8 0.0 copy-done.5
  61.8 0.0 copy-start
  61.8 1.3 %carry_in.1 = bf16[16,64,128]{2,1,0:T(8,128)(2,1)} custom-call(s32[2]{0:T(128)S(1)} %pad_add_fusion.pos_ref, bf16[4,1104,128]{2,1,0:T(8,128)(2,1)S(1)} %all_to_all.21.rows_ref.q_ref, bf16[16,80,128]{2,1,0:T(8,128)(2,1)S(1)} %all_to_all.20.got_ref), custom_call_target="tpu_custom_call" | custom-call | flops 1 | bytes 1 | tf_op jit(solution)/shard_map/carry_in/pallas_call | solution.py:304
  63.2 17.9 %all-to-all-start.2 = ((bf16[16,64,128]{2,1,0:T(8,128)(2,1)}), bf16[16,64,128]{2,1,0:T(8,128)(2,1)S(1)}, u32[]{:S(2)}, u32[]{:S(2)}) async-start(bf16[16,64,128]{2,1,0:T(8,128)(2,1)} %carry_in.1), calls=%async_computation.2 | async-start | bytes 524288 | tf_op jit(solution)/shard_map/all_to_all | solution.py:319
  81.1 2.8 %all-gather.4.cloned.1.call-done.kv_hbm = bf16[16,344,128]{2,1,0:T(8,128)(2,1)} async-done(((bf16[2,344,128]{2,1,0:T(8,128)(2,1)}), bf16[16,344,128]{2,1,0:T(8,128)(2,1)}) %all-gather.4.cloned.1.call-update) | async-done | bytes 1409040 | tf_op jit(solution)/shard_map/all_gather | solution.py:261
  83.9 0.0 copy-done
  83.9 14.8 %attend.1 = bf16[4,1056,128]{2,1,0:T(8,128)(2,1)} custom-call(s32[2]{0:T(128)} %copy-done.5, bf16[4,1104,128]{2,1,0:T(8,128)(2,1)} %copy-done, bf16[16,344,128]{2,1,0:T(8,128)(2,1)} %all-gather.4.cloned.1.call-done.kv_hbm), custom_call_target="tpu_custom_call" | custom-call | flops 6442450944 | bytes 4194304 | tf_op jit(solution)/shard_map/attend/pallas_call | solution.py:321
  98.8 0.0 copy-start.1
  98.8 0.0 copy-start.2
  98.8 0.0 copy-start.3
  98.8 0.0 copy-start.6
  98.8 0.0 all-to-all-done.2
  98.8 3.7 %all-to-all-start.3 = ((bf16[4,1056,128]{2,1,0:T(8,128)(2,1)}), bf16[4,1056,128]{2,1,0:T(8,128)(2,1)S(1)}, u32[]{:S(2)}, u32[]{:S(2)}) async-start(bf16[4,1056,128]{2,1,0:T(8,128)(2,1)} %attend.1), calls=%async_computation.3 | async-start | bytes 2162688 | tf_op jit(solution)/shard_map/all_to_all | solution.py:339
  102.5 0.0 copy-done.1
  102.5 0.0 copy-done.2
  102.5 0.0 copy-done.3
  102.5 0.3 mix.1
  102.9 15.3 %psum.7 = f32[1,128]{1,0:T(1,128)S(1)} all-reduce(f32[1,128]{1,0:T(1,128)S(1)} %get-tuple-element.34), channel_id=1, replica_groups=mesh['ctx'=64,'head'=8] {'head'}, use_global_device_ids=true, to_apply=%region_0.0 | all-reduce | flops 128 | bytes 1024 | tf_op jit(solution)/shard_map/psum | solution.py:351
  118.1 0.0 copy-done.6
  118.1 0.9 fusion.1
  119.0 0.0 all-to-all-done.3.got_ref
  119.0 1.3 %merge.1 = bf16[1024,128]{1,0:T(8,128)(2,1)} custom-call(bf16[4,1056,128]{2,1,0:T(8,128)(2,1)S(1)} %all-to-all-done.3.got_ref), custom_call_target="tpu_custom_call" | custom-call | flops 1048576 | bytes 2097152 | tf_op jit(solution)/shard_map/merge/pallas_call | solution.py:356
  (4 shorter events, 0.0 us)
Async XLA Ops:
  7.2 76.8 %all-gather.4.cloned.1.call-start = ((), (), s32[]{:S(2)}) async-start(), calls=%async_computation.4 | async-start | bytes 1585152 | tf_op jit(solution)/shard_map/all_gather | solution.py:261
  13.3 48.5 %copy-start.5 = (s32[2]{0:T(128)}, s32[2]{0:T(128)S(1)}, u32[]{:S(2)}) copy-start(s32[2]{0:T(128)S(1)} %pad_add_fusion.pos_ref) | copy-start | bytes 28
  17.3 30.2 %copy-start.4 = (bf16[128,8,128]{2,1,0:T(8,128)(2,1)S(1)}, bf16[128,8,128]{2,1,0:T(8,128)(2,1)}, u32[]{:S(2)}) copy-start(bf16[128,8,128]{2,1,0:T(8,128)(2,1)} %param.13) | copy-start | bytes 786436
  61.8 22.1 %copy-start = (bf16[4,1104,128]{2,1,0:T(8,128)(2,1)}, bf16[4,1104,128]{2,1,0:T(8,128)(2,1)S(1)}, u32[]{:S(2)}) copy-start(bf16[4,1104,128]{2,1,0:T(8,128)(2,1)S(1)} %all_to_all.21.rows_ref.q_ref) | copy-start | bytes 3391492
  63.2 35.6 %all-to-all-start.2 = ((bf16[16,64,128]{2,1,0:T(8,128)(2,1)}), bf16[16,64,128]{2,1,0:T(8,128)(2,1)S(1)}, u32[]{:S(2)}, u32[]{:S(2)}) async-start(bf16[16,64,128]{2,1,0:T(8,128)(2,1)} %carry_in.1), calls=%async_computation.2 | async-start | bytes 524288 | tf_op jit(solution)/shard_map/all_to_all | solution.py:319
  98.8 3.7 %copy-start.1 = (f32[8,128,128]{2,1,0:T(8,128)S(1)}, f32[8,128,128]{2,1,0:T(8,128)}, u32[]{:S(2)}) copy-start(f32[8,128,128]{2,1,0:T(8,128)} %get-tuple-element.23.inner_ref) | copy-start | bytes 1572868
  98.8 3.7 %copy-start.2 = (bf16[8,128,128]{2,1,0:T(8,128)(2,1)S(1)}, bf16[8,128,128]{2,1,0:T(8,128)(2,1)}, u32[]{:S(2)}) copy-start(bf16[8,128,128]{2,1,0:T(8,128)(2,1)} %get-tuple-element.22.act_ref) | copy-start | bytes 786436
  98.8 3.7 %copy-start.3 = (f32[128,128]{1,0:T(8,128)S(1)}, f32[128,128]{1,0:T(8,128)}, u32[]{:S(2)}) copy-start(f32[128,128]{1,0:T(8,128)} %get-tuple-element.24.ecum_ref) | copy-start | bytes 196612
  98.8 19.3 %copy-start.6 = (f32[8,128]{1,0:T(8,128)S(1)}, f32[8,128]{1,0:T(8,128)}, u32[]{:S(2)}) copy-start(f32[8,128]{1,0:T(8,128)} %param.12) | copy-start | bytes 12292
  98.8 20.2 %all-to-all-start.3 = ((bf16[4,1056,128]{2,1,0:T(8,128)(2,1)}), bf16[4,1056,128]{2,1,0:T(8,128)(2,1)S(1)}, u32[]{:S(2)}, u32[]{:S(2)}) async-start(bf16[4,1056,128]{2,1,0:T(8,128)(2,1)} %attend.1), calls=%async_computation.3 | async-start | bytes 2162688 | tf_op jit(solution)/shard_map/all_to_all | solution.py:339
Sparse Core Ops, SparseCore 0:
  13.5 70.4 all-gather.3

commit v4 on v3

--- a/solution.py
+++ b/solution.py
@@ -12,7 +12,7 @@
 ROWS = TOK * HEADS
 Y, Z = 4, 16
 SLICE = ROWS // Z
-STATE_ROWS = SLICE + 16
+STATE_ROWS = SLICE + 8
 STAT_ROWS = 32
 SPARE = 88
 KV_ROWS = 2 * TOK + SPARE
@@ -36,7 +36,7 @@
 
 def scalar_rows(x):
     high, mid, low = (part.astype(F32) for part in split3(x))
-    row = lax.broadcasted_iota(jnp.int32, (16, 128), 0)
+    row = lax.broadcasted_iota(jnp.int32, (8, 128), 0)
     out = jnp.where(row == 0, high, jnp.where(row == 1, mid, jnp.where(row == 2, low, 0.0)))
     return out.astype(BF16)
 
@@ -304,13 +304,8 @@
     pay = pl.pallas_call(
         carry_kernel,
         out_shape=shape(Z, SLICE, 128),
-        grid=(1,),
-        in_specs=[
-            SM,
-            pl.BlockSpec((Y, STATE_ROWS, 128), lambda i: (0, 0, 0)),
-            pl.BlockSpec((Z, STATE_ROWS, 128), lambda i: (0, 0, 0)),
-        ],
-        out_specs=pl.BlockSpec((Z, SLICE, 128), lambda i: (0, 0, 0)),
+        in_specs=[SM, VM, VM],
+        out_specs=VM,
         compiler_params=params(),
         cost_estimate=cost(1, 1),
         name="carry_in",

time: 128 us -> 126 us (0.984)
  blocking collectives: 64.7 us -> 62.9 us
    all_to_all x1, blocking collectives: 30.2 us -> 28.6 us  [local(): got = lax.all_to_all(pay, 'ctx', 0, 0, axis_index_groups=Z_GROUPS)]
  transfers between devices with their start and end apart: 3 -> 3, of which waited for: 1 -> 1; matrix products, arithmetic and copies ran while one was open for 1% -> 1% of each run, Pallas kernels for 16% -> 17%
where the time goes in v4:
time: 126 us; the launch traced here: 125 us
  blocking collectives  62.9 us (50%)
  Pallas kernels  22 us (17%)
  starting transfers between devices  20.6 us (16%)
  between operations  14.2 us (11%)
  waiting for transfers between devices  3.21 us (3%)
  other arithmetic  1.88 us (1%)
    all_to_all x1, blocking collectives, local(): got = lax.all_to_all(pay, 'ctx', 0, 0, axis_index_groups=Z_GROUPS)  28.6 us
    all_to_all x1, starting transfers between devices, local(): prior = lax.all_to_all(pay, 'ctx', 0, 0, axis_index_groups=Z_GROUPS)  16.9 us
    pallas_call x1, Pallas kernels, local(): pl.pallas_call(attend_kernel, out_shape=shape(Y, STAT_ROWS + ROWS, HD), i...  14.9 us
    psum x1, blocking collectives, local(): total = lax.psum(squares, 'head')  14.6 us
    all_to_all x1, blocking collectives, local(): queries = lax.all_to_all(pay, 'ctx', 0, 0, axis_index_groups=Y_GROUPS)  14.5 us
    all_gather x1, blocking collectives, local(): kv = lax.all_gather(kv, 'ctx', axis_index_groups=PAIR_GROUPS)  5.12 us
    pallas_call x1, Pallas kernels, local(): pl.pallas_call(local_kernel, out_shape=(shape(Z, STATE_ROWS, 128), shape(...  3.89 us
    all_to_all x1, starting transfers between devices, local(): got = lax.all_to_all(pay, 'ctx', 0, 0, axis_index_groups=Y_GROUPS)  3.66 us
  transfers between devices with their start and end apart: 3, of which 1 were waited for; matrix products, arithmetic and copies ran while one was open for 1% of the time, Pallas kernels for 17%

profile of v4, /device:TPU:1, one launch (start us, length us, event | category | flops | bytes accessed | tf_op | source)
XLA Modules:
  0.0 124.7 jit_solution(14240014539453660024)
XLA Ops:
  7.2 0.0 all-gather.4.cloned.1.call-start
  7.2 0.9 maximum_maximum_fusion
  8.1 5.1 %all-gather = bf16[688,128]{1,0:T(8,128)(2,1)} all-gather(bf16[344,128]{1,0:T(8,128)(2,1)S(1)} %maximum_maximum_fusion), channel_id=2, replica_groups={{0,8},{16,24},{32,40},{48,56},{64,72},{80,88},{96,104},{112,120},{128,1..., dimensions={0}, use_global_device_ids=true | all-gather | bytes 264192 | tf_op jit(solution)/shard_map/all_gather | solution.py:257
  13.3 0.1 pad_add_fusion.pos_ref
  13.3 0.0 copy-start.5
  13.3 0.0 all-gather.4.cloned.1.call-update
  13.4 3.9 %local_part.1 = (bf16[16,72,128]{2,1,0:T(8,128)(2,1)}, f32[8,128,128]{2,1,0:T(8,128)}, bf16[8,128,128]{2,1,0:T(8,128)(2,1)}, f32[128,128]{1,0:T(8,128)}) custom-call(bf16[1024,128]{1,0:T(8,128)(2,1)} %bitcast.22, bf16[1024,128]{1,0:T(8,128)(2,1)} %bitcast.23, bf16[1024,128]{1,0:T(8,128)(2,1)} %bitcast.24, f32[8,128]{1,0:T(8,128)} %decay_hbm.1), custom_call_target="tpu_custom_call" | custom-call | flops 1 | bytes 1 | tf_op jit(solution)/shard_map/local_part/pallas_call | solution.py:262
  17.3 0.0 copy-start.3
  17.3 28.6 %all_to_all.20.got_ref = bf16[16,72,128]{2,1,0:T(8,128)(2,1)S(1)} all-to-all(bf16[16,72,128]{2,1,0:T(8,128)(2,1)} %keep.1), channel_id=1, replica_groups={{0,8,16,24,32,40,48,56,64,72,80,88,96,104,112,120},{128,136,144,152,160..., dimensions={0} | all-to-all | bytes 589824 | tf_op jit(solution)/shard_map/all_to_all | solution.py:290
  45.9 0.0 copy-done.3
  45.9 0.2 row_scan.1
  46.1 14.5 %all_to_all.21.rows_ref.q_ref = bf16[4,1096,128]{2,1,0:T(8,128)(2,1)S(1)} all-to-all(bf16[4,1096,128]{2,1,0:T(8,128)(2,1)S(1)} %row_scan.1), channel_id=1, replica_groups={{0,128,256,384},{8,136,264,392},{16,144,272,400},{24,152,280,408},{32,1..., dimensions={0} | all-to-all | bytes 2244608 | tf_op jit(solution)/shard_map/all_to_all | solution.py:302
  60.6 0.0 copy-done.5
  60.6 0.0 copy-start
  60.6 1.3 %carry_in.1 = bf16[16,64,128]{2,1,0:T(8,128)(2,1)} custom-call(s32[2]{0:T(128)S(1)} %pad_add_fusion.pos_ref, bf16[4,1096,128]{2,1,0:T(8,128)(2,1)S(1)} %all_to_all.21.rows_ref.q_ref, bf16[16,72,128]{2,1,0:T(8,128)(2,1)S(1)} %all_to_all.20.got_ref), custom_call_target="tpu_custom_call" | custom-call | flops 1 | bytes 1 | tf_op jit(solution)/shard_map/carry_in/pallas_call | solution.py:304
  61.9 16.9 %all-to-all-start.2 = ((bf16[16,64,128]{2,1,0:T(8,128)(2,1)}), bf16[16,64,128]{2,1,0:T(8,128)(2,1)S(1)}, u32[]{:S(2)}, u32[]{:S(2)}) async-start(bf16[16,64,128]{2,1,0:T(8,128)(2,1)} %carry_in.1), calls=%async_computation.2 | async-start | bytes 524288 | tf_op jit(solution)/shard_map/all_to_all | solution.py:314
  78.8 3.2 %all-gather.4.cloned.1.call-done.kv_hbm = bf16[16,344,128]{2,1,0:T(8,128)(2,1)} async-done(((bf16[2,344,128]{2,1,0:T(8,128)(2,1)}), bf16[16,344,128]{2,1,0:T(8,128)(2,1)}) %all-gather.4.cloned.1.call-update) | async-done | bytes 1409040 | tf_op jit(solution)/shard_map/all_gather | solution.py:261
  82.0 0.0 copy-done
  82.0 14.9 %attend.1 = bf16[4,1056,128]{2,1,0:T(8,128)(2,1)} custom-call(s32[2]{0:T(128)} %copy-done.5, bf16[4,1096,128]{2,1,0:T(8,128)(2,1)} %copy-done, bf16[16,344,128]{2,1,0:T(8,128)(2,1)} %all-gather.4.cloned.1.call-done.kv_hbm), custom_call_target="tpu_custom_call" | custom-call | flops 6442450944 | bytes 4194304 | tf_op jit(solution)/shard_map/attend/pallas_call | solution.py:316
  96.9 0.0 copy-start.1
  96.9 0.0 copy-start.2
  96.9 0.0 copy-start.4
  96.9 0.0 copy-start.6
  96.9 0.0 all-to-all-done.2
  97.0 3.7 %all-to-all-start.3 = ((bf16[4,1056,128]{2,1,0:T(8,128)(2,1)}), bf16[4,1056,128]{2,1,0:T(8,128)(2,1)S(1)}, u32[]{:S(2)}, u32[]{:S(2)}) async-start(bf16[4,1056,128]{2,1,0:T(8,128)(2,1)} %attend.1), calls=%async_computation.3 | async-start | bytes 2162688 | tf_op jit(solution)/shard_map/all_to_all | solution.py:334
  100.6 0.0 copy-done.1
  100.6 0.0 copy-done.2
  100.6 0.0 copy-done.4
  100.7 0.3 mix.1
  101.0 14.6 %psum.7 = f32[1,128]{1,0:T(1,128)S(1)} all-reduce(f32[1,128]{1,0:T(1,128)S(1)} %get-tuple-element.34), channel_id=1, replica_groups=mesh['ctx'=64,'head'=8] {'head'}, use_global_device_ids=true, to_apply=%region_0.0 | all-reduce | flops 128 | bytes 1024 | tf_op jit(solution)/shard_map/psum | solution.py:346
  115.6 0.0 copy-done.6
  115.6 0.9 fusion.1
  116.5 0.0 all-to-all-done.3.got_ref
  116.6 1.3 %merge.1 = bf16[1024,128]{1,0:T(8,128)(2,1)} custom-call(bf16[4,1056,128]{2,1,0:T(8,128)(2,1)S(1)} %all-to-all-done.3.got_ref), custom_call_target="tpu_custom_call" | custom-call | flops 1048576 | bytes 2097152 | tf_op jit(solution)/shard_map/merge/pallas_call | solution.py:351
  (4 shorter events, 0.0 us)
Async XLA Ops:
  7.2 74.9 %all-gather.4.cloned.1.call-start = ((), (), s32[]{:S(2)}) async-start(), calls=%async_computation.4 | async-start | bytes 1585152 | tf_op jit(solution)/shard_map/all_gather | solution.py:261
  13.3 47.3 %copy-start.5 = (s32[2]{0:T(128)}, s32[2]{0:T(128)S(1)}, u32[]{:S(2)}) copy-start(s32[2]{0:T(128)S(1)} %pad_add_fusion.pos_ref) | copy-start | bytes 28
  17.3 28.6 %copy-start.3 = (bf16[128,8,128]{2,1,0:T(8,128)(2,1)S(1)}, bf16[128,8,128]{2,1,0:T(8,128)(2,1)}, u32[]{:S(2)}) copy-start(bf16[128,8,128]{2,1,0:T(8,128)(2,1)} %param.13) | copy-start | bytes 786436
  60.6 21.4 %copy-start = (bf16[4,1096,128]{2,1,0:T(8,128)(2,1)}, bf16[4,1096,128]{2,1,0:T(8,128)(2,1)S(1)}, u32[]{:S(2)}) copy-start(bf16[4,1096,128]{2,1,0:T(8,128)(2,1)S(1)} %all_to_all.21.rows_ref.q_ref) | copy-start | bytes 3366916
  61.9 35.0 %all-to-all-start.2 = ((bf16[16,64,128]{2,1,0:T(8,128)(2,1)}), bf16[16,64,128]{2,1,0:T(8,128)(2,1)S(1)}, u32[]{:S(2)}, u32[]{:S(2)}) async-start(bf16[16,64,128]{2,1,0:T(8,128)(2,1)} %carry_in.1), calls=%async_computation.2 | async-start | bytes 524288 | tf_op jit(solution)/shard_map/all_to_all | solution.py:314
  96.9 3.7 %copy-start.1 = (f32[8,128,128]{2,1,0:T(8,128)S(1)}, f32[8,128,128]{2,1,0:T(8,128)}, u32[]{:S(2)}) copy-start(f32[8,128,128]{2,1,0:T(8,128)} %get-tuple-element.23.inner_ref) | copy-start | bytes 1572868
  96.9 3.7 %copy-start.2 = (bf16[8,128,128]{2,1,0:T(8,128)(2,1)S(1)}, bf16[8,128,128]{2,1,0:T(8,128)(2,1)}, u32[]{:S(2)}) copy-start(bf16[8,128,128]{2,1,0:T(8,128)(2,1)} %get-tuple-element.22.act_ref) | copy-start | bytes 786436
  96.9 3.7 %copy-start.4 = (f32[128,128]{1,0:T(8,128)S(1)}, f32[128,128]{1,0:T(8,128)}, u32[]{:S(2)}) copy-start(f32[128,128]{1,0:T(8,128)} %get-tuple-element.24.ecum_ref) | copy-start | bytes 196612
  96.9 18.7 %copy-start.6 = (f32[8,128]{1,0:T(8,128)S(1)}, f32[8,128]{1,0:T(8,128)}, u32[]{:S(2)}) copy-start(f32[8,128]{1,0:T(8,128)} %param.12) | copy-start | bytes 12292
  97.0 19.6 %all-to-all-start.3 = ((bf16[4,1056,128]{2,1,0:T(8,128)(2,1)}), bf16[4,1056,128]{2,1,0:T(8,128)(2,1)S(1)}, u32[]{:S(2)}, u32[]{:S(2)}) async-start(bf16[4,1056,128]{2,1,0:T(8,128)(2,1)} %attend.1), calls=%async_computation.3 | async-start | bytes 2162688 | tf_op jit(solution)/shard_map/all_to_all | solution.py:334
Sparse Core Ops, SparseCore 0:
  13.5 68.4 all-gather.3
